TPU v7x, 32 devices: a whole 2x2x4 slice. The times are simulated.
32 devices in a mesh: ang: 4 (over y, x), rad: 8 (over z, core).
Axes of the slice: x: 2, y: 2, z: 4, core: 2. Of those that a mesh axis runs over, the one named last changes fastest.
Arguments:
- right_side: float32 [1024, 4096], P('rad', 'ang'), may hold values from -6 to 7
- guess: float32 [1024, 4096], P('rad', 'ang'), may hold values from -6 to 6
Outputs:
- solution: float32 [1024, 4096], P('rad', 'ang')
- residual: float32 [1024, 4096], P('rad', 'ang')
All inputs are finite; a program needn't handle non-finite values.
Results may differ from a plain program's by a relative error of at most 0.007.
Values sent between devices are 32-bit elements; how exact they have to be, the bound alone decides.
No kernel may reach another device: no remote copies, remote signals or barrier semaphores. Data moves between devices by JAX's collectives and lax.ppermute only.
A program may use at most 128 MiB of HBM per device.

v0:
```python
import math

import jax
import jax.numpy as jnp
from jax import lax
from jax.sharding import PartitionSpec as P

LEVELS = 8
PRE = 2
POST = 2
COARSE_SWEEPS = 8


def padded_2(x, sides, width, wrap):
    for axis, dim in sides:
        size, length = (lax.axis_size(axis), x.shape[dim])
        up = [(i, (i + 1) % size) for i in range(size if wrap else size - 1)]
        down = [(j, i) for i, j in up]
        last = lax.slice_in_dim(x, length - width, length, axis=dim)
        leading = lax.slice_in_dim(x, 0, width, axis=dim)
        before = lax.ppermute(last, axis, up)
        after = lax.ppermute(leading, axis, down)
        x = jnp.concatenate([before, x, after], axis=dim)
    return x


def coefficients(row_float, spacing):
    radius = 1.0 + (row_float + 0.5) * spacing
    offset_ratio = 0.5 * spacing / radius
    outward = 1.0 + offset_ratio
    inward = 1.0 - offset_ratio
    angular = 1.0 / (radius * radius)
    centre = 2.0 + 2.0 * angular
    return (outward, inward, angular, centre)


def relax_cells(padded, source, stencil, chosen):
    outward, inward, angular, centre = stencil
    middle = padded[1:-1, 1:-1]
    updated = (
        source
        + outward * padded[2:, 1:-1]
        + inward * padded[:-2, 1:-1]
        + angular * (padded[1:-1, 2:] + padded[1:-1, :-2])
    ) / centre
    return jnp.where(chosen, updated, middle)


def apply_operator(padded, stencil):
    outward, inward, angular, centre = stencil
    middle = padded[1:-1, 1:-1]
    return (
        centre * middle
        - outward * padded[2:, 1:-1]
        - inward * padded[:-2, 1:-1]
        - angular * (padded[1:-1, 2:] + padded[1:-1, :-2])
    )


def restrict_grid(padded):
    height = padded.shape[0] - 2
    breadth = padded.shape[1] - 2
    row_sum = (
        padded[0:height:2]
        + 3.0 * padded[1 : height + 1 : 2]
        + 3.0 * padded[2 : height + 2 : 2]
        + padded[3 : height + 3 : 2]
    ) * 0.125
    col_sum = (
        row_sum[:, 0:breadth:2]
        + 3.0 * row_sum[:, 1 : breadth + 1 : 2]
        + 3.0 * row_sum[:, 2 : breadth + 2 : 2]
        + row_sum[:, 3 : breadth + 3 : 2]
    ) * 0.125
    return 4.0 * col_sum


def prolong_grid(padded):
    centre_rep = jnp.repeat(padded[1:-1], 2, axis=0)
    below_rep = jnp.repeat(padded[:-2], 2, axis=0)
    above_rep = jnp.repeat(padded[2:], 2, axis=0)
    row_ids = jnp.arange(centre_rep.shape[0], dtype=jnp.int32)[:, None]
    stretched = 0.75 * centre_rep + 0.25 * jnp.where(row_ids % 2 == 0, below_rep, above_rep)
    mid_cols = jnp.repeat(stretched[:, 1:-1], 2, axis=1)
    left_cols = jnp.repeat(stretched[:, :-2], 2, axis=1)
    right_cols = jnp.repeat(stretched[:, 2:], 2, axis=1)
    col_ids = jnp.arange(mid_cols.shape[1], dtype=jnp.int32)[None, :]
    return 0.75 * mid_cols + 0.25 * jnp.where(col_ids % 2 == 0, left_cols, right_cols)


def wrap_pad(values, margin):
    values = jnp.pad(values, ((0, 0), (margin, margin)), mode="wrap")
    return jnp.pad(values, ((margin, margin), (0, 0)))


def cycle_local(level_at, iterate, source):
    height, breadth = source.shape
    spacing = 2.0 * math.pi / breadth
    row_ids = jnp.arange(height, dtype=jnp.int32)[:, None]
    col_ids = jnp.arange(breadth, dtype=jnp.int32)[None, :]
    stencil = coefficients(row_ids.astype(jnp.float32), spacing)
    red_cells = (row_ids + col_ids) % 2 == 0
    black_cells = jnp.logical_not(red_cells)

    def colour_sweep(values):
        values = relax_cells(wrap_pad(values, 1), source, stencil, red_cells)
        return relax_cells(wrap_pad(values, 1), source, stencil, black_cells)

    if level_at == LEVELS - 1:
        for _ in range(COARSE_SWEEPS):
            iterate = colour_sweep(iterate)
        return iterate
    for _ in range(PRE):
        iterate = colour_sweep(iterate)
    remainder = source - apply_operator(wrap_pad(iterate, 1), stencil)
    coarse_source = restrict_grid(wrap_pad(remainder, 1))
    correction = cycle_local(level_at + 1, jnp.zeros_like(coarse_source), coarse_source)
    iterate = iterate + prolong_grid(wrap_pad(correction, 1))
    for _ in range(POST):
        iterate = colour_sweep(iterate)
    return iterate


def extend_halo(values, margin):
    values = padded_2(values, (("ang", 1),), margin, True)
    return padded_2(values, (("rad", 0),), margin, False)


def block_grid(height, breadth, lead):
    row_start = lax.axis_index("rad") * height - lead
    col_start = lax.axis_index("ang") * breadth - lead
    row_ids = row_start + jnp.arange(height + 2 * lead, dtype=jnp.int32)[:, None]
    col_ids = col_start + jnp.arange(breadth + 2 * lead, dtype=jnp.int32)[None, :]
    spacing = 2.0 * math.pi / (breadth * lax.axis_size("ang"))
    stencil = coefficients(row_ids.astype(jnp.float32), spacing)
    red_cells = (row_ids + col_ids) % 2 == 0
    inside = jnp.logical_and(row_ids >= 0, row_ids < height * lax.axis_size("rad"))
    return (stencil, red_cells, inside)


def cycle_spread(level_at, iterate, source, gather_level, layers):
    height, breadth = source.shape
    stencil, red_cells, inside = block_grid(height, breadth, 0)
    black_cells = jnp.logical_not(red_cells)
    loop_stencil, loop_red, loop_inside = block_grid(height, breadth, 1)
    loop_chosen = jnp.logical_and(loop_red, loop_inside)
    loop_source = extend_halo(source, 1)

    def colour_sweep(values):
        loop_cells = relax_cells(extend_halo(values, 2), loop_source, loop_stencil, loop_chosen)
        return relax_cells(loop_cells, source, stencil, black_cells)

    for _ in range(PRE):
        iterate = colour_sweep(iterate)
    remainder = source - apply_operator(extend_halo(iterate, 1), stencil)
    coarse_source = restrict_grid(extend_halo(remainder, 1))
    if level_at + 1 == gather_level:
        coarse_height, coarse_breadth = coarse_source.shape
        whole_grid = lax.all_gather(coarse_source, "ang", axis=1, tiled=True)
        whole_grid = lax.all_gather(whole_grid, "rad", axis=0, tiled=True)
        whole_fix = cycle_local(level_at + 1, jnp.zeros_like(whole_grid), whole_grid)
        correction = lax.dynamic_slice(
            whole_fix,
            (lax.axis_index("rad") * coarse_height, lax.axis_index("ang") * coarse_breadth),
            (coarse_height, coarse_breadth),
        )
    else:
        correction = cycle_spread(
            level_at + 1, jnp.zeros_like(coarse_source), coarse_source, gather_level, layers
        )
    iterate = iterate + prolong_grid(extend_halo(correction, 1))
    for _ in range(POST):
        iterate = colour_sweep(iterate)
    return iterate


def local(right_side, guess):
    gather_level = 5
    layers = 2
    solution = cycle_spread(0, guess, right_side, gather_level, layers)
    height, breadth = right_side.shape
    stencil, red_cells, inside = block_grid(height, breadth, 0)
    residual = right_side - apply_operator(extend_halo(solution, 1), stencil)
    return (solution, residual)


def solution(mesh):
    placed = (P("rad", "ang"), P("rad", "ang"))
    return jax.shard_map(
        local,
        mesh=mesh,
        in_specs=placed,
        out_specs=(P("rad", "ang"), P("rad", "ang")),
        check_vma=False,
    )
```

profile of v0, /device:TPU:1, one launch (start us, length us, event | category | flops | bytes accessed | tf_op | source)
XLA Modules:
  0.0 608.2 jit_solution(2268981053462445065)
XLA Ops:
  33.7 4.0 collective-permute-start.6
  37.7 3.5 collective-permute-start.7
  41.3 2.4 collective-permute-start.2
  45.7 2.9 collective-permute-done.3
  58.1 3.6 collective-permute-start.11
  69.7 2.3 collective-permute-start.14
  72.0 4.7 collective-permute-start.15
  83.2 5.6 collective-permute-start.18
  98.5 4.5 slice.2377
  103.0 4.5 slice.2378
  107.5 4.5 slice.2379
  112.0 4.5 slice.2380
  122.3 3.6 collective-permute-start.27
  126.0 2.3 collective-permute-start.22
  130.5 2.7 collective-permute-done.23
  141.1 3.7 collective-permute-start.31
  153.1 5.4 collective-permute-start.35
  165.4 5.9 collective-permute-start.38
  186.6 3.6 collective-permute-start.47
  192.5 2.2 collective-permute-start.43
  200.0 2.4 collective-permute-start.49
  205.5 3.6 collective-permute-start.51
  214.9 2.2 collective-permute-start.54
  217.1 5.3 collective-permute-start.55
  227.5 5.7 collective-permute-start.58
  243.2 4.6 collective-permute-start.67
  249.8 2.4 collective-permute-start.63
  262.5 3.6 collective-permute-start.71
  271.7 2.3 collective-permute-start.74
  274.0 5.3 collective-permute-start.75
  283.6 5.6 collective-permute-start.78
  293.1 3.6 collective-permute-start.87
  302.1 3.9 collective-permute-start.82
  308.0 2.9 collective-permute-done.83
  317.8 3.6 collective-permute-start.91
  330.5 3.9 collective-permute-start.95
  338.7 5.6 collective-permute-start.98
  346.4 2.8 collective-permute-done.99
  349.9 6.8 %all-gather = f32[4,32,4]{1,2,0:T(4,128)S(1)} all-gather(f32[1,32,4]{1,2,0:T(4,128)S(1)} %multiply_bitcast_fusion), channel_id=1, replica_groups=mesh['ang'=4,'rad'=8] {'ang'}, dimensions={0}, use_global_device_ids=true | all-gather | bytes 2560 | tf_op jit(solution)/shard_map/all_gather | solution.py:159
  356.8 13.9 %all-gather.1 = f32[8,4,128]{2,1,0:T(4,128)S(1)} all-gather(f32[1,4,128]{2,1,0:T(4,128)S(1)} %bitcast.85), channel_id=1, replica_groups=mesh['ang'=4,'rad'=8] {'rad'}, dimensions={0}, use_global_device_ids=true | all-gather | bytes 18432 | tf_op jit(solution)/shard_map/all_gather | solution.py:160
  389.9 4.3 collective-permute-start.102
  396.2 2.9 collective-permute-done.103
  406.6 3.6 collective-permute-start.107
  414.8 2.2 collective-permute-start.110
  417.0 5.3 collective-permute-start.111
  427.8 5.6 collective-permute-start.114
  435.3 2.9 collective-permute-done.115
  444.6 3.6 collective-permute-start.119
  453.8 2.2 collective-permute-start.122
  456.0 5.3 collective-permute-start.123
  466.0 5.6 collective-permute-start.126
  473.6 2.9 collective-permute-done.127
  484.1 3.6 collective-permute-start.131
  494.8 5.3 collective-permute-start.135
  505.9 5.6 collective-permute-start.138
  511.5 2.2 collective-permute-start.139
  513.9 2.6 collective-permute-done.139
  523.8 3.6 collective-permute-start.143
  536.0 5.4 collective-permute-start.147
  546.9 5.6 collective-permute-start.150
  554.8 2.6 collective-permute-done.151
  571.2 3.8 collective-permute-start.155
  585.3 5.0 collective-permute-start.159
  599.8 5.6 collective-permute-start.163
  (1048 shorter events, 338.9 us)
Async XLA Ops:
  1.7 31.2 %collective-permute-start.4 = (f32[128,2]{1,0:T(8,128)S(1)}, f32[128,2]{1,0:T(8,128)S(1)}, u32[]{:S(2)}, u32[]{:S(2)}) collective-permute-start(f32[128,2]{1,0:T(8,128)S(1)} %get-tuple-element.63), channel_id=1, source_target_pairs={{0,8},{8,16},{16,24},{24,0},{1,9},{9,17},{17,25},{25,1},{2,10},{10... | collective-permute-start | bytes 3080 | tf_op jit(solution)/shard_map/ppermute | solution.py:21
  3.7 29.1 %collective-permute-start.5 = (f32[128,2]{1,0:T(8,128)S(1)}, f32[128,2]{1,0:T(8,128)S(1)}, u32[]{:S(2)}, u32[]{:S(2)}) collective-permute-start(f32[128,2]{1,0:T(8,128)S(1)} %get-tuple-element.62), channel_id=1, source_target_pairs={{8,0},{16,8},{24,16},{0,24},{9,1},{17,9},{25,17},{1,25},{10,2},{18... | collective-permute-start | bytes 3080 | tf_op jit(solution)/shard_map/ppermute | solution.py:22
  5.7 23.9 %collective-permute-start = (f32[128,1]{1,0:T(8,128)S(1)}, f32[128,1]{1,0:T(8,128)S(1)}, u32[]{:S(2)}, u32[]{:S(2)}) collective-permute-start(f32[128,1]{1,0:T(8,128)S(1)} %get-tuple-element.61), channel_id=1, source_target_pairs={{0,8},{8,16},{16,24},{24,0},{1,9},{9,17},{17,25},{25,1},{2,10},{10... | collective-permute-start | bytes 1544 | tf_op jit(solution)/shard_map/ppermute | solution.py:21
  6.2 25.6 %collective-permute-start.1 = (f32[128,1]{1,0:T(8,128)S(1)}, f32[128,1]{1,0:T(8,128)S(1)}, u32[]{:S(2)}, u32[]{:S(2)}) collective-permute-start(f32[128,1]{1,0:T(8,128)S(1)} %get-tuple-element.60), channel_id=1, source_target_pairs={{8,0},{16,8},{24,16},{0,24},{9,1},{17,9},{25,17},{1,25},{10,2},{18... | collective-permute-start | bytes 1544 | tf_op jit(solution)/shard_map/ppermute | solution.py:22
  8.7 107.9 %collective-permute-start.24 = (f32[64,2]{1,0:T(8,128)}, f32[64,2]{1,0:T(8,128)S(1)}, u32[]{:S(2)}, u32[]{:S(2)}) collective-permute-start(f32[64,2]{1,0:T(8,128)} %broadcast.2046), channel_id=1, source_target_pairs={{0,8},{8,16},{16,24},{24,0},{1,9},{9,17},{17,25},{25,1},{2,10},{10... | collective-permute-start | bytes 1544 | tf_op jit(solution)/shard_map/ppermute | solution.py:21
  29.6 87.8 %collective-permute-start.25 = (f32[64,2]{1,0:T(8,128)}, f32[64,2]{1,0:T(8,128)S(1)}, u32[]{:S(2)}, u32[]{:S(2)}) collective-permute-start(f32[64,2]{1,0:T(8,128)} %broadcast.2046), channel_id=1, source_target_pairs={{8,0},{16,8},{24,16},{0,24},{9,1},{17,9},{25,17},{1,25},{10,2},{18... | collective-permute-start | bytes 1544 | tf_op jit(solution)/shard_map/ppermute | solution.py:22
  32.4 133.0 %collective-permute-start.44 = (f32[32,2]{1,0:T(8,128)}, f32[32,2]{1,0:T(8,128)}, u32[]{:S(2)}, u32[]{:S(2)}) collective-permute-start(f32[32,2]{1,0:T(8,128)} %broadcast.2055), channel_id=1, source_target_pairs={{0,8},{8,16},{16,24},{24,0},{1,9},{9,17},{17,25},{25,1},{2,10},{10... | collective-permute-start | bytes 776 | tf_op jit(solution)/shard_map/ppermute | solution.py:21
  33.7 7.5 %collective-permute-start.6 = (f32[2,1028]{1,0:T(2,128)S(1)}, f32[2,1028]{1,0:T(2,128)S(1)}, u32[]{:S(2)}, u32[]{:S(2)}) collective-permute-start(f32[2,1028]{1,0:T(2,128)S(1)} %get-tuple-element.47), channel_id=1, source_target_pairs={{1,0},{2,1},{3,2},{4,3},{5,4},{6,5},{7,6},{9,8},{10,9},{11,10},{12... | collective-permute-start | bytes 24680 | tf_op jit(solution)/shard_map/ppermute | solution.py:22
  37.7 6.0 collective-permute-start.7
  56.2 6.1 %collective-permute-start.10 = (f32[2,1028]{1,0:T(2,128)S(1)}, f32[2,1028]{1,0:T(2,128)S(1)}, u32[]{:S(2)}, u32[]{:S(2)}) collective-permute-start(f32[2,1028]{1,0:T(2,128)S(1)} %get-tuple-element.43), channel_id=1, source_target_pairs={{1,0},{2,1},{3,2},{4,3},{5,4},{6,5},{7,6},{9,8},{10,9},{11,10},{12... | collective-permute-start | bytes 24680 | tf_op jit(solution)/shard_map/ppermute | solution.py:22
  69.7 7.6 %collective-permute-start.14 = (f32[1,1026]{1,0:T(1,128)S(1)}, f32[1,1026]{1,0:T(1,128)S(1)}, u32[]{:S(2)}, u32[]{:S(2)}) collective-permute-start(f32[1,1026]{1,0:T(1,128)S(1)} %get-tuple-element.40), channel_id=1, source_target_pairs={{1,0},{2,1},{3,2},{4,3},{5,4},{6,5},{7,6},{9,8},{10,9},{11,10},{12... | collective-permute-start | bytes 12320 | tf_op jit(solution)/shard_map/ppermute | solution.py:22
  83.2 8.2 %collective-permute-start.18 = (f32[1,1026]{1,0:T(1,128)S(1)}, f32[1,1026]{1,0:T(1,128)S(1)}, u32[]{:S(2)}, u32[]{:S(2)}) collective-permute-start(f32[1,1026]{1,0:T(1,128)S(1)} %get-tuple-element.38), channel_id=1, source_target_pairs={{0,1},{1,2},{2,3},{3,4},{4,5},{5,6},{6,7},{8,9},{9,10},{10,11},{11... | collective-permute-start | bytes 12320 | tf_op jit(solution)/shard_map/ppermute | solution.py:21
  91.5 79.8 %collective-permute-start.45 = (f32[32,2]{1,0:T(8,128)}, f32[32,2]{1,0:T(8,128)}, u32[]{:S(2)}, u32[]{:S(2)}) collective-permute-start(f32[32,2]{1,0:T(8,128)} %broadcast.2055), channel_id=1, source_target_pairs={{8,0},{16,8},{24,16},{0,24},{9,1},{17,9},{25,17},{1,25},{10,2},{18... | collective-permute-start | bytes 776 | tf_op jit(solution)/shard_map/ppermute | solution.py:22
  94.4 138.8 %collective-permute-start.64 = (f32[16,2]{1,0:T(8,128)}, f32[16,2]{1,0:T(8,128)}, u32[]{:S(2)}, u32[]{:S(2)}) collective-permute-start(f32[16,2]{1,0:T(8,128)} %broadcast.2070), channel_id=1, source_target_pairs={{0,8},{8,16},{16,24},{24,0},{1,9},{9,17},{17,25},{25,1},{2,10},{10... | collective-permute-start | bytes 392 | tf_op jit(solution)/shard_map/ppermute | solution.py:21
  120.3 5.7 collective-permute-start.26
  122.3 6.1 collective-permute-start.27
  139.2 5.6 collective-permute-start.30
  150.9 7.6 %collective-permute-start.34 = (f32[1,514]{1,0:T(1,128)S(1)}, f32[1,514]{1,0:T(1,128)S(1)}, u32[]{:S(2)}, u32[]{:S(2)}) collective-permute-start(f32[1,514]{1,0:T(1,128)S(1)} %get-tuple-element.73), channel_id=1, source_target_pairs={{1,0},{2,1},{3,2},{4,3},{5,4},{6,5},{7,6},{9,8},{10,9},{11,10},{12... | collective-permute-start | bytes 6176 | tf_op jit(solution)/shard_map/ppermute | solution.py:22
  153.1 6.1 %collective-permute-start.35 = (f32[1,514]{1,0:T(1,128)S(1)}, f32[1,514]{1,0:T(1,128)S(1)}, u32[]{:S(2)}, u32[]{:S(2)}) collective-permute-start(f32[1,514]{1,0:T(1,128)S(1)} %get-tuple-element.74), channel_id=1, source_target_pairs={{0,1},{1,2},{2,3},{3,4},{4,5},{5,6},{6,7},{8,9},{9,10},{10,11},{11... | collective-permute-start | bytes 6176 | tf_op jit(solution)/shard_map/ppermute | solution.py:21
  163.2 72.0 %collective-permute-start.65 = (f32[16,2]{1,0:T(8,128)}, f32[16,2]{1,0:T(8,128)S(1)}, u32[]{:S(2)}, u32[]{:S(2)}) collective-permute-start(f32[16,2]{1,0:T(8,128)} %broadcast.2070), channel_id=1, source_target_pairs={{8,0},{16,8},{24,16},{0,24},{9,1},{17,9},{25,17},{1,25},{10,2},{18... | collective-permute-start | bytes 392 | tf_op jit(solution)/shard_map/ppermute | solution.py:22
  163.9 115.4 %collective-permute-start.84 = (f32[8,2]{1,0:T(8,128)S(1)}, f32[8,2]{1,0:T(8,128)S(1)}, u32[]{:S(2)}, u32[]{:S(2)}) collective-permute-start(f32[8,2]{1,0:T(8,128)S(1)} %broadcast.2087), channel_id=1, source_target_pairs={{0,8},{8,16},{16,24},{24,0},{1,9},{9,17},{17,25},{25,1},{2,10},{10... | collective-permute-start | bytes 200 | tf_op jit(solution)/shard_map/ppermute | solution.py:21
  165.4 8.9 %collective-permute-start.38 = (f32[1,514]{1,0:T(1,128)S(1)}, f32[1,514]{1,0:T(1,128)S(1)}, u32[]{:S(2)}, u32[]{:S(2)}) collective-permute-start(f32[1,514]{1,0:T(1,128)S(1)} %get-tuple-element.83), channel_id=1, source_target_pairs={{0,1},{1,2},{2,3},{3,4},{4,5},{5,6},{6,7},{8,9},{9,10},{10,11},{11... | collective-permute-start | bytes 6176 | tf_op jit(solution)/shard_map/ppermute | solution.py:21
  184.7 5.7 collective-permute-start.46
  186.6 5.9 collective-permute-start.47
  203.6 5.6 collective-permute-start.50
  214.9 7.6 %collective-permute-start.54 = (f32[1,258]{1,0:T(1,128)S(1)}, f32[1,258]{1,0:T(1,128)S(1)}, u32[]{:S(2)}, u32[]{:S(2)}) collective-permute-start(f32[1,258]{1,0:T(1,128)S(1)} %get-tuple-element.108), channel_id=1, source_target_pairs={{1,0},{2,1},{3,2},{4,3},{5,4},{6,5},{7,6},{9,8},{10,9},{11,10},{12... | collective-permute-start | bytes 3104 | tf_op jit(solution)/shard_map/ppermute | solution.py:22
  217.1 6.1 collective-permute-start.55
  226.8 52.5 %collective-permute-start.85 = (f32[8,2]{1,0:T(8,128)S(1)}, f32[8,2]{1,0:T(8,128)S(1)}, u32[]{:S(2)}, u32[]{:S(2)}) collective-permute-start(f32[8,2]{1,0:T(8,128)S(1)} %broadcast.2087), channel_id=1, source_target_pairs={{8,0},{16,8},{24,16},{0,24},{9,1},{17,9},{25,17},{1,25},{10,2},{18... | collective-permute-start | bytes 200 | tf_op jit(solution)/shard_map/ppermute | solution.py:22
  227.5 10.4 %collective-permute-start.58 = (f32[1,258]{1,0:T(1,128)S(1)}, f32[1,258]{1,0:T(1,128)S(1)}, u32[]{:S(2)}, u32[]{:S(2)}) collective-permute-start(f32[1,258]{1,0:T(1,128)S(1)} %get-tuple-element.118), channel_id=1, source_target_pairs={{0,1},{1,2},{2,3},{3,4},{4,5},{5,6},{6,7},{8,9},{9,10},{10,11},{11... | collective-permute-start | bytes 3104 | tf_op jit(solution)/shard_map/ppermute | solution.py:21
  235.9 13.9 %collective-permute-start.66 = (f32[2,132]{1,0:T(2,128)S(1)}, f32[2,132]{1,0:T(2,128)S(1)}, u32[]{:S(2)}, u32[]{:S(2)}) collective-permute-start(f32[2,132]{1,0:T(2,128)S(1)} %get-tuple-element.172), channel_id=1, source_target_pairs={{1,0},{2,1},{3,2},{4,3},{5,4},{6,5},{7,6},{9,8},{10,9},{11,10},{12... | collective-permute-start | bytes 3176 | tf_op jit(solution)/shard_map/ppermute | solution.py:22
  241.1 6.7 %collective-permute-start.61 = (f32[16,1]{1,0:T(8,128)S(1)}, f32[16,1]{1,0:T(8,128)S(1)}, u32[]{:S(2)}, u32[]{:S(2)}) collective-permute-start(f32[16,1]{1,0:T(8,128)S(1)} %get-tuple-element.221), channel_id=1, source_target_pairs={{8,0},{16,8},{24,16},{0,24},{9,1},{17,9},{25,17},{1,25},{10,2},{18... | collective-permute-start | bytes 200 | tf_op jit(solution)/shard_map/ppermute | solution.py:22
  243.2 9.0 %collective-permute-start.67 = (f32[2,132]{1,0:T(2,128)S(1)}, f32[2,132]{1,0:T(2,128)S(1)}, u32[]{:S(2)}, u32[]{:S(2)}) collective-permute-start(f32[2,132]{1,0:T(2,128)S(1)} %get-tuple-element.171), channel_id=1, source_target_pairs={{0,1},{1,2},{2,3},{3,4},{4,5},{5,6},{6,7},{8,9},{9,10},{10,11},{11... | collective-permute-start | bytes 3176 | tf_op jit(solution)/shard_map/ppermute | solution.py:21
  260.6 5.6 collective-permute-start.70
  271.7 7.6 %collective-permute-start.74 = (f32[1,130]{1,0:T(1,128)S(1)}, f32[1,130]{1,0:T(1,128)S(1)}, u32[]{:S(2)}, u32[]{:S(2)}) collective-permute-start(f32[1,130]{1,0:T(1,128)S(1)} %get-tuple-element.165), channel_id=1, source_target_pairs={{1,0},{2,1},{3,2},{4,3},{5,4},{6,5},{7,6},{9,8},{10,9},{11,10},{12... | collective-permute-start | bytes 1568 | tf_op jit(solution)/shard_map/ppermute | solution.py:22
  274.0 6.0 collective-permute-start.75
  283.6 13.1 %collective-permute-start.78 = (f32[1,130]{1,0:T(1,128)S(1)}, f32[1,130]{1,0:T(1,128)S(1)}, u32[]{:S(2)}, u32[]{:S(2)}) collective-permute-start(f32[1,130]{1,0:T(1,128)S(1)} %get-tuple-element.196), channel_id=1, source_target_pairs={{0,1},{1,2},{2,3},{3,4},{4,5},{5,6},{6,7},{8,9},{9,10},{10,11},{11... | collective-permute-start | bytes 1568 | tf_op jit(solution)/shard_map/ppermute | solution.py:21
  289.3 7.5 %collective-permute-start.79 = (f32[1,130]{1,0:T(1,128)S(1)}, f32[1,130]{1,0:T(1,128)S(1)}, u32[]{:S(2)}, u32[]{:S(2)}) collective-permute-start(f32[1,130]{1,0:T(1,128)S(1)} %get-tuple-element.197), channel_id=1, source_target_pairs={{1,0},{2,1},{3,2},{4,3},{5,4},{6,5},{7,6},{9,8},{10,9},{11,10},{12... | collective-permute-start | bytes 1568 | tf_op jit(solution)/shard_map/ppermute | solution.py:22
  291.2 16.7 %collective-permute-start.86 = (f32[2,68]{1,0:T(2,128)S(1)}, f32[2,68]{1,0:T(2,128)S(1)}, u32[]{:S(2)}, u32[]{:S(2)}) collective-permute-start(f32[2,68]{1,0:T(2,128)S(1)} %get-tuple-element.322), channel_id=1, source_target_pairs={{1,0},{2,1},{3,2},{4,3},{5,4},{6,5},{7,6},{9,8},{10,9},{11,10},{12... | collective-permute-start | bytes 1640 | tf_op jit(solution)/shard_map/ppermute | solution.py:22
  293.1 14.8 %collective-permute-start.87 = (f32[2,68]{1,0:T(2,128)S(1)}, f32[2,68]{1,0:T(2,128)S(1)}, u32[]{:S(2)}, u32[]{:S(2)}) collective-permute-start(f32[2,68]{1,0:T(2,128)S(1)} %get-tuple-element.321), channel_id=1, source_target_pairs={{0,1},{1,2},{2,3},{3,4},{4,5},{5,6},{6,7},{8,9},{9,10},{10,11},{11... | collective-permute-start | bytes 1640 | tf_op jit(solution)/shard_map/ppermute | solution.py:21
  302.1 5.9 collective-permute-start.82
  315.9 7.8 %collective-permute-start.90 = (f32[2,68]{1,0:T(2,128)S(1)}, f32[2,68]{1,0:T(2,128)S(1)}, u32[]{:S(2)}, u32[]{:S(2)}) collective-permute-start(f32[2,68]{1,0:T(2,128)S(1)} %get-tuple-element.314), channel_id=1, source_target_pairs={{1,0},{2,1},{3,2},{4,3},{5,4},{6,5},{7,6},{9,8},{10,9},{11,10},{12... | collective-permute-start | bytes 1640 | tf_op jit(solution)/shard_map/ppermute | solution.py:22
  317.8 5.9 collective-permute-start.91
  328.4 6.1 %collective-permute-start.94 = (f32[1,66]{1,0:T(1,128)S(1)}, f32[1,66]{1,0:T(1,128)S(1)}, u32[]{:S(2)}, u32[]{:S(2)}) collective-permute-start(f32[1,66]{1,0:T(1,128)S(1)} %get-tuple-element.309), channel_id=1, source_target_pairs={{1,0},{2,1},{3,2},{4,3},{5,4},{6,5},{7,6},{9,8},{10,9},{11,10},{12... | collective-permute-start | bytes 800 | tf_op jit(solution)/shard_map/ppermute | solution.py:22
  338.7 7.7 %collective-permute-start.98 = (f32[1,66]{1,0:T(1,128)S(1)}, f32[1,66]{1,0:T(1,128)S(1)}, u32[]{:S(2)}, u32[]{:S(2)}) collective-permute-start(f32[1,66]{1,0:T(1,128)S(1)} %get-tuple-element.303), channel_id=1, source_target_pairs={{0,1},{1,2},{2,3},{3,4},{4,5},{5,6},{6,7},{8,9},{9,10},{10,11},{11... | collective-permute-start | bytes 800 | tf_op jit(solution)/shard_map/ppermute | solution.py:21
  389.9 6.3 %collective-permute-start.102 = (f32[1,34]{1,0:T(1,128)S(1)}, f32[1,34]{1,0:T(1,128)S(1)}, u32[]{:S(2)}, u32[]{:S(2)}) collective-permute-start(f32[1,34]{1,0:T(1,128)S(1)} %get-tuple-element.324), channel_id=1, source_target_pairs={{0,1},{1,2},{2,3},{3,4},{4,5},{5,6},{6,7},{8,9},{9,10},{10,11},{11... | collective-permute-start | bytes 416 | tf_op jit(solution)/shard_map/ppermute | solution.py:21
  414.8 7.5 %collective-permute-start.110 = (f32[2,68]{1,0:T(2,128)S(1)}, f32[2,68]{1,0:T(2,128)S(1)}, u32[]{:S(2)}, u32[]{:S(2)}) collective-permute-start(f32[2,68]{1,0:T(2,128)S(1)} %get-tuple-element.229), channel_id=1, source_target_pairs={{1,0},{2,1},{3,2},{4,3},{5,4},{6,5},{7,6},{9,8},{10,9},{11,10},{12... | collective-permute-start | bytes 1640 | tf_op jit(solution)/shard_map/ppermute | solution.py:22
  417.0 6.0 collective-permute-start.111
  427.8 7.5 %collective-permute-start.114 = (f32[1,66]{1,0:T(1,128)S(1)}, f32[1,66]{1,0:T(1,128)S(1)}, u32[]{:S(2)}, u32[]{:S(2)}) collective-permute-start(f32[1,66]{1,0:T(1,128)S(1)} %get-tuple-element.225), channel_id=1, source_target_pairs={{0,1},{1,2},{2,3},{3,4},{4,5},{5,6},{6,7},{8,9},{9,10},{10,11},{11... | collective-permute-start | bytes 800 | tf_op jit(solution)/shard_map/ppermute | solution.py:21
  453.8 7.5 %collective-permute-start.122 = (f32[2,132]{1,0:T(2,128)S(1)}, f32[2,132]{1,0:T(2,128)S(1)}, u32[]{:S(2)}, u32[]{:S(2)}) collective-permute-start(f32[2,132]{1,0:T(2,128)S(1)} %get-tuple-element.162), channel_id=1, source_target_pairs={{1,0},{2,1},{3,2},{4,3},{5,4},{6,5},{7,6},{9,8},{10,9},{11,10},{12... | collective-permute-start | bytes 3176 | tf_op jit(solution)/shard_map/ppermute | solution.py:22
  456.0 6.1 collective-permute-start.123
  466.0 7.6 %collective-permute-start.126 = (f32[1,130]{1,0:T(1,128)S(1)}, f32[1,130]{1,0:T(1,128)S(1)}, u32[]{:S(2)}, u32[]{:S(2)}) collective-permute-start(f32[1,130]{1,0:T(1,128)S(1)} %get-tuple-element.174), channel_id=1, source_target_pairs={{0,1},{1,2},{2,3},{3,4},{4,5},{5,6},{6,7},{8,9},{9,10},{10,11},{11... | collective-permute-start | bytes 1568 | tf_op jit(solution)/shard_map/ppermute | solution.py:21
  482.2 5.6 collective-permute-start.130
  492.7 7.5 %collective-permute-start.134 = (f32[2,260]{1,0:T(2,128)S(1)}, f32[2,260]{1,0:T(2,128)S(1)}, u32[]{:S(2)}, u32[]{:S(2)}) collective-permute-start(f32[2,260]{1,0:T(2,128)S(1)} %get-tuple-element.105), channel_id=1, source_target_pairs={{1,0},{2,1},{3,2},{4,3},{5,4},{6,5},{7,6},{9,8},{10,9},{11,10},{12... | collective-permute-start | bytes 6248 | tf_op jit(solution)/shard_map/ppermute | solution.py:22
  494.8 6.0 collective-permute-start.135
  505.9 7.9 %collective-permute-start.138 = (f32[1,258]{1,0:T(1,128)S(1)}, f32[1,258]{1,0:T(1,128)S(1)}, u32[]{:S(2)}, u32[]{:S(2)}) collective-permute-start(f32[1,258]{1,0:T(1,128)S(1)} %get-tuple-element.117), channel_id=1, source_target_pairs={{0,1},{1,2},{2,3},{3,4},{4,5},{5,6},{6,7},{8,9},{9,10},{10,11},{11... | collective-permute-start | bytes 3104 | tf_op jit(solution)/shard_map/ppermute | solution.py:21
  521.8 5.6 collective-permute-start.142
  533.8 7.6 %collective-permute-start.146 = (f32[2,516]{1,0:T(2,128)S(1)}, f32[2,516]{1,0:T(2,128)S(1)}, u32[]{:S(2)}, u32[]{:S(2)}) collective-permute-start(f32[2,516]{1,0:T(2,128)S(1)} %get-tuple-element.70), channel_id=1, source_target_pairs={{1,0},{2,1},{3,2},{4,3},{5,4},{6,5},{7,6},{9,8},{10,9},{11,10},{12... | collective-permute-start | bytes 12392 | tf_op jit(solution)/shard_map/ppermute | solution.py:22
  536.0 6.1 %collective-permute-start.147 = (f32[2,516]{1,0:T(2,128)S(1)}, f32[2,516]{1,0:T(2,128)S(1)}, u32[]{:S(2)}, u32[]{:S(2)}) collective-permute-start(f32[2,516]{1,0:T(2,128)S(1)} %get-tuple-element.69), channel_id=1, source_target_pairs={{0,1},{1,2},{2,3},{3,4},{4,5},{5,6},{6,7},{8,9},{9,10},{10,11},{11... | collective-permute-start | bytes 12392 | tf_op jit(solution)/shard_map/ppermute | solution.py:21
  546.9 7.9 %collective-permute-start.150 = (f32[1,514]{1,0:T(1,128)S(1)}, f32[1,514]{1,0:T(1,128)S(1)}, u32[]{:S(2)}, u32[]{:S(2)}) collective-permute-start(f32[1,514]{1,0:T(1,128)S(1)} %get-tuple-element.82), channel_id=1, source_target_pairs={{0,1},{1,2},{2,3},{3,4},{4,5},{5,6},{6,7},{8,9},{9,10},{10,11},{11... | collective-permute-start | bytes 6176 | tf_op jit(solution)/shard_map/ppermute | solution.py:21
  569.2 5.8 collective-permute-start.154
  583.3 7.1 %collective-permute-start.158 = (f32[2,1028]{1,0:T(2,128)S(1)}, f32[2,1028]{1,0:T(2,128)S(1)}, u32[]{:S(2)}, u32[]{:S(2)}) collective-permute-start(f32[2,1028]{1,0:T(2,128)S(1)} %get-tuple-element.35), channel_id=1, source_target_pairs={{1,0},{2,1},{3,2},{4,3},{5,4},{6,5},{7,6},{9,8},{10,9},{11,10},{12... | collective-permute-start | bytes 24680 | tf_op jit(solution)/shard_map/ppermute | solution.py:22
  585.3 5.8 collective-permute-start.159
  597.9 7.6 %collective-permute-start.162 = (f32[1,1026]{1,0:T(1,128)S(1)}, f32[1,1026]{1,0:T(1,128)S(1)}, u32[]{:S(2)}, u32[]{:S(2)}) collective-permute-start(f32[1,1026]{1,0:T(1,128)S(1)} %get-tuple-element.32), channel_id=1, source_target_pairs={{1,0},{2,1},{3,2},{4,3},{5,4},{6,5},{7,6},{9,8},{10,9},{11,10},{12... | collective-permute-start | bytes 12320 | tf_op jit(solution)/shard_map/ppermute | solution.py:22
  599.8 6.4 %collective-permute-start.163 = (f32[1,1026]{1,0:T(1,128)S(1)}, f32[1,1026]{1,0:T(1,128)S(1)}, u32[]{:S(2)}, u32[]{:S(2)}) collective-permute-start(f32[1,1026]{1,0:T(1,128)S(1)} %get-tuple-element.33), channel_id=1, source_target_pairs={{0,1},{1,2},{2,3},{3,4},{4,5},{5,6},{6,7},{8,9},{9,10},{10,11},{11... | collective-permute-start | bytes 12320 | tf_op jit(solution)/shard_map/ppermute | solution.py:21
  (205 other events, 1704.5 us)
where the time goes:
time: 618 us; the launch traced here: 608 us
  starting transfers between devices  362 us (59%)
  waiting for transfers between devices  101 us (16%)
  other arithmetic  60.6 us (10%)
  local copies, waits for them, and re-layouts  58.5 us (9%)
  blocking collectives  20.7 us (3%)
    ppermute x82, starting transfers between devices, padded_2(): before = lax.ppermute(last, axis, up)  231 us
    ppermute x82, starting transfers between devices, padded_2(): after = lax.ppermute(leading, axis, down)  131 us
    ppermute x82, waiting for transfers between devices, padded_2(): before = lax.ppermute(last, axis, up)  55.4 us
    ppermute x82, waiting for transfers between devices, padded_2(): after = lax.ppermute(leading, axis, down)  45.4 us
    select_n x72, other arithmetic, relax_cells(): return jnp.where(chosen, updated, middle)  17.7 us
    all_gather x1, blocking collectives, cycle_spread(): whole_grid = lax.all_gather(whole_grid, 'rad', axis=0, tiled=True)  13.9 us
  transfers between devices with their start and end apart: 164, of which 88 were waited for; matrix products, arithmetic and copies ran while one was open for 12% of the time, Pallas kernels for 0%

commit v1 on v0

v1 whole, which is shorter than its diff:
```python
import math

import jax
import jax.numpy as jnp
from jax import lax
from jax.experimental import pallas as pl
from jax.experimental.pallas import tpu as pltpu
from jax.sharding import PartitionSpec as P

LEVELS = 8
PRE = 2
POST = 2
COARSE_SWEEPS = 8
SPREAD = 3
PAD = 8
UP = 8
LANES = 128
SIDE = 64
HIGH = lax.Precision.HIGHEST


def iota(shape, dim):
    return lax.broadcasted_iota(jnp.int32, shape, dim)


def dot(a, b):
    return lax.dot_general(
        a, b, (((1,), (0,)), ((), ())), precision=HIGH, preferred_element_type=jnp.float32
    )


def wide(x, breadth):
    return x if breadth == LANES else jnp.concatenate([x] * (breadth // LANES), axis=1)


def chunk_of(rows, breadth):
    units = rows // 8
    best = 1
    for n in range(1, units + 1):
        if units % n == 0 and n * 8 * breadth <= 20 * 1024:
            best = n
    return 8 * best


class Level:
    def __init__(self, v, g, cf, spacing, total, first):
        self.v, self.g, self.cf = v, g, cf
        self.rows, self.breadth = g.shape
        self.spacing, self.total, self.first = spacing, total, first
        self.n = chunk_of(self.rows, self.breadth)

    def fill(self):
        shape = (self.rows, LANES)
        ids = self.first + iota(shape, 0)
        radius = 1.0 + (ids.astype(jnp.float32) + 0.5) * self.spacing
        ratio = 0.5 * self.spacing / radius
        angular = 1.0 / (radius * radius)
        centre = 2.0 + 2.0 * angular
        inside = jnp.logical_and(ids >= 0, ids < self.total)
        self.cf[pl.ds(0 * self.rows, self.rows), :] = 1.0 + ratio
        self.cf[pl.ds(1 * self.rows, self.rows), :] = 1.0 - ratio
        self.cf[pl.ds(2 * self.rows, self.rows), :] = angular
        self.cf[pl.ds(3 * self.rows, self.rows), :] = centre
        self.cf[pl.ds(4 * self.rows, self.rows), :] = jnp.where(inside, 1.0 / centre, 0.0)
        zero = jnp.zeros((PAD, self.breadth), jnp.float32)
        self.v[pl.ds(0, PAD), :] = zero
        self.v[pl.ds(PAD + self.rows, PAD), :] = zero

    def loop(self, body):
        steps = self.rows // self.n
        if steps == 1:
            body(0)
        else:
            def step(k, carry):
                body(pl.multiple_of(k * self.n, 8))
                return carry

            lax.fori_loop(0, steps, step, 0)

    def coef(self, which, b):
        return wide(self.cf[pl.ds(which * self.rows + b, self.n), :], self.breadth)

    def parity(self):
        shape = (self.n, LANES)
        return wide(((iota(shape, 0) + iota(shape, 1)) & 1).astype(jnp.float32), self.breadth)

    def neighbours(self, b):
        near = self.v[pl.ds(b, self.n + 2 * PAD), :]
        mid = near[PAD : PAD + self.n]
        below = near[PAD - 1 : PAD - 1 + self.n]
        above = near[PAD + 1 : PAD + 1 + self.n]
        sides = pltpu.roll(mid, 1, 1) + pltpu.roll(mid, self.breadth - 1, 1)
        total = (
            self.coef(0, b) * above + self.coef(1, b) * below + self.coef(2, b) * sides
        )
        return mid, total

    def half(self, colour):
        chosen = self.parity() == float(colour)

        def body(b):
            mid, total = self.neighbours(b)
            updated = (self.g[pl.ds(b, self.n), :] + total) * self.coef(4, b)
            self.v[pl.ds(b + PAD, self.n), :] = jnp.where(chosen, updated, mid)

        self.loop(body)

    def sweeps(self, count):
        for _ in range(count):
            self.half(0)
            self.half(1)

    def sweeps_from_zero(self, count):
        red = self.parity() == 0.0

        def body(b):
            updated = self.g[pl.ds(b, self.n), :] * self.coef(4, b)
            self.v[pl.ds(b + PAD, self.n), :] = jnp.where(red, updated, 0.0)

        self.loop(body)
        self.half(1)
        self.sweeps(count - 1)

    def residual(self, out):
        def body(b):
            mid, total = self.neighbours(b)
            s = self.g[pl.ds(b, self.n), :] - (self.coef(3, b) * mid - total)
            out[pl.ds(b, self.n), :] = jnp.where(self.coef(4, b) != 0.0, s, 0.0)

        self.loop(body)

    def add(self, p):
        inside = wide(self.cf[pl.ds(4 * self.rows, self.rows), :], self.breadth) != 0.0
        at = pl.ds(PAD, self.rows)
        self.v[at, :] = self.v[at, :] + jnp.where(inside, p, 0.0)


def one(cond):
    return jnp.where(cond, 1.0, 0.0).astype(jnp.float32)


def restricted(s, halo, period):
    rows, breadth = s.shape
    shape = (rows // 2, rows)
    gap = iota(shape, 1) - 2 * iota(shape, 0)
    weights = jnp.where(
        jnp.logical_or(gap == 0, gap == 1),
        0.375,
        jnp.where(jnp.logical_or(gap == -1, gap == 2), 0.125, 0.0),
    ).astype(jnp.float32)
    t = dot(weights, s[...])
    u = 0.5 * (
        pltpu.roll(t, 1, 1)
        + 3.0 * t
        + 3.0 * pltpu.roll(t, breadth - 1, 1)
        + pltpu.roll(t, breadth - 2, 1)
    )
    own = breadth - (LANES if halo else 0)
    tiles = []
    if own >= 2 * LANES:
        shape = (2 * LANES, LANES)
        pick = one(iota(shape, 0) == 2 * iota(shape, 1))
        for k in range(own // (2 * LANES)):
            tiles.append(dot(u[:, 2 * LANES * k : 2 * LANES * (k + 1)], pick))
    else:
        shape = (LANES, LANES)
        pick = one(iota(shape, 0) == 2 * (iota(shape, 1) % (period // 2)))
        tiles.append(dot(u, pick))
    if halo:
        shape = (LANES, LANES)
        j, i = iota(shape, 0), iota(shape, 1)
        right = jnp.logical_and(j == 2 * i, j < SIDE)
        left = jnp.logical_and(j == 2 * i - LANES, j >= SIDE)
        tiles.append(dot(u[:, own:], one(jnp.logical_or(right, left))))
    return tiles[0] if len(tiles) == 1 else jnp.concatenate(tiles, axis=1)


def prolonged(e, rows, shift, halo, fine_period):
    breadth = e.shape[1]
    a = 0.75 * e + 0.25 * pltpu.roll(e, 1, 1)
    b = 0.75 * e + 0.25 * pltpu.roll(e, breadth - 1, 1)
    own = breadth - (LANES if halo else 0)
    tiles = []

    def pair(k):
        at = slice(LANES * k, LANES * (k + 1))
        return jnp.concatenate([a[:, at], b[:, at]], axis=1)

    if fine_period > LANES:
        shape = (2 * LANES, 2 * LANES)
        i, j = iota(shape, 0), iota(shape, 1)
        spread = one(j == jnp.where(i < LANES, 2 * i, 2 * (i - LANES) + 1))
        for k in range(own // LANES):
            tiles.append(dot(pair(k), spread))
    else:
        shape = (2 * LANES, LANES)
        i, j = iota(shape, 0), iota(shape, 1) % fine_period
        spread = one(j == jnp.where(i < LANES, 2 * i, 2 * (i - LANES) + 1))
        tiles.append(dot(pair(0), spread))
    if halo:
        shape = (2 * LANES, LANES)
        i, j = iota(shape, 0), iota(shape, 1)
        lane = i % LANES
        source = jnp.where(j < SIDE, j // 2, j // 2 + SIDE)
        spread = one(jnp.logical_and(lane == source, i // LANES == j % 2))
        tiles.append(dot(pair(own // LANES), spread))
    p = tiles[0] if len(tiles) == 1 else jnp.concatenate(tiles, axis=1)
    shape = (rows, e.shape[0])
    i, c = iota(shape, 0), iota(shape, 1)
    near = i // 2 + shift
    far = near + jnp.where(i % 2 == 0, -1, 1)
    weights = jnp.where(c == near, 0.75, jnp.where(c == far, 0.25, 0.0)).astype(jnp.float32)
    return dot(weights, p)


def down_kernel(height, total, spacings, place, v, hv, g, hg, top, bottom, *refs):
    outs, scratch = refs[: 2 * SPREAD + 1], refs[2 * SPREAD + 1 :]
    halo = UP << SPREAD
    breadth = v.shape[1]
    rows = height + 2 * halo
    vb, gb = scratch[0], scratch[1]
    at = pl.ds(PAD + halo, height)
    vb[at, pl.ds(0, breadth)] = v[...]
    vb[at, pl.ds(breadth, LANES)] = hv[...]
    vb[pl.ds(PAD, halo), :] = top[pl.ds(0, halo), :]
    vb[pl.ds(PAD + halo + height, halo), :] = bottom[pl.ds(0, halo), :]
    at = pl.ds(halo, height)
    gb[at, pl.ds(0, breadth)] = g[...]
    gb[at, pl.ds(breadth, LANES)] = hg[...]
    gb[pl.ds(0, halo), :] = top[pl.ds(halo, halo), :]
    gb[pl.ds(halo + height, halo), :] = bottom[pl.ds(halo, halo), :]
    for l in range(SPREAD):
        vb, gb, cf, s = scratch[4 * l : 4 * l + 4]
        edge = halo >> l
        own = height >> l
        level = Level(vb, gb, cf, spacings[l], total >> l, place[0] * own - edge)
        level.fill()
        if l == 0:
            level.sweeps(PRE)
        else:
            level.sweeps_from_zero(PRE)
        outs[2 * l][...] = vb[pl.ds(PAD + edge - UP, own + 2 * UP), :]
        outs[2 * l + 1][...] = gb[pl.ds(edge - UP, own + 2 * UP), :]
        level.residual(s)
        coarse = restricted(s, True, None)
        if l + 1 < SPREAD:
            scratch[4 * (l + 1) + 1][...] = coarse
        else:
            edge, own = edge // 2, own // 2
            outs[2 * SPREAD][...] = coarse[edge : edge + own, : outs[2 * SPREAD].shape[1]]


def up_kernel(height, total, spacings, sizes, place, gathered, *refs):
    ins, refs = refs[: 2 * SPREAD], refs[2 * SPREAD :]
    out_v, out_s, scratch = refs[0], refs[1], refs[2:]
    rads, angs = sizes
    whole = []
    for l in range(SPREAD, LEVELS):
        v, g, cf, s = scratch[4 * (l - SPREAD) : 4 * (l - SPREAD) + 4]
        whole.append((Level(v, g, cf, spacings[l], total >> l, 0), s))
    g = whole[0][0].g
    piece = gathered.shape[1:]
    for r in range(rads):
        for a in range(angs):
            g[pl.ds(r * piece[0], piece[0]), pl.ds(a * piece[1], piece[1])] = gathered[r * angs + a]

    def period(l):
        return (piece[1] * angs) >> (l - SPREAD)

    for l in range(SPREAD, LEVELS):
        level, s = whole[l - SPREAD]
        level.fill()
        if l == LEVELS - 1:
            level.sweeps_from_zero(COARSE_SWEEPS)
        else:
            level.sweeps_from_zero(PRE)
            level.residual(s)
            whole[l + 1 - SPREAD][0].g[...] = restricted(s, False, period(l))
    for l in range(LEVELS - 2, SPREAD - 1, -1):
        level, s = whole[l - SPREAD]
        coarse = whole[l + 1 - SPREAD][0]
        e = coarse.v[pl.ds(PAD, coarse.rows), :]
        level.add(prolonged(e, level.rows, 0, False, period(l)))
        level.sweeps(POST)
    v = whole[0][0].v
    start = place[1] * piece[1]
    across = piece[1] * angs
    at = pl.ds(pl.multiple_of(place[0] * piece[0], 8), piece[0] + 2 * UP)
    after = pl.multiple_of(lax.rem(start + piece[1], across), LANES)
    before = pl.multiple_of(lax.rem(start + across - LANES, across), LANES)
    tile = (piece[0] + 2 * UP, LANES)
    halo = jnp.where(iota(tile, 1) < SIDE, v[at, pl.ds(after, LANES)], v[at, pl.ds(before, LANES)])
    own = v[at, pl.ds(pl.multiple_of(start, LANES), piece[1])]
    e = jnp.concatenate([own, halo], axis=1)
    base = 4 * (LEVELS - SPREAD)
    for l in range(SPREAD - 1, -1, -1):
        v, cf = scratch[base + 2 * l : base + 2 * l + 2]
        own = height >> l
        level = Level(v, ins[2 * l + 1], cf, spacings[l], total >> l, place[0] * own - UP)
        level.fill()
        v[pl.ds(PAD, level.rows), :] = ins[2 * l][...]
        level.add(prolonged(e, level.rows, UP // 2, True, 2 * LANES))
        level.sweeps(POST)
        e = v[pl.ds(PAD, level.rows), :]
    s = scratch[-1]
    level.residual(s)
    breadth = out_v.shape[1]
    out_v[...] = v[pl.ds(PAD + UP, height), pl.ds(0, breadth)]
    out_s[...] = s[pl.ds(UP, height), pl.ds(0, breadth)]


def f32(*shape):
    return jax.ShapeDtypeStruct(shape, jnp.float32)


def vmem(*shape):
    return pltpu.VMEM(shape, jnp.float32)


def local(right_side, guess):
    height, breadth = right_side.shape
    rads, angs = lax.axis_size("rad"), lax.axis_size("ang")
    total = height * rads
    spacings = [2.0 * math.pi / ((breadth * angs) >> l) for l in range(LEVELS)]
    halo = UP << SPREAD
    up = [(i, (i + 1) % angs) for i in range(angs)]
    down = [(j, i) for i, j in up]
    first = jnp.concatenate([guess[:, :SIDE], right_side[:, :SIDE]], axis=1)
    last = jnp.concatenate([guess[:, -SIDE:], right_side[:, -SIDE:]], axis=1)
    after = lax.ppermute(first, "ang", down)
    before = lax.ppermute(last, "ang", up)
    halo_v = jnp.concatenate([after[:, :SIDE], before[:, :SIDE]], axis=1)
    halo_g = jnp.concatenate([after[:, SIDE:], before[:, SIDE:]], axis=1)

    def edge(at):
        top = jnp.concatenate([guess[at], halo_v[at]], axis=1)
        low = jnp.concatenate([right_side[at], halo_g[at]], axis=1)
        return jnp.concatenate([top, low], axis=0)

    up = [(i, i + 1) for i in range(rads - 1)]
    down = [(j, i) for i, j in up]
    above = lax.ppermute(edge(slice(-halo, None)), "rad", up)
    below = lax.ppermute(edge(slice(0, halo)), "rad", down)
    place = jnp.stack([lax.axis_index("rad"), lax.axis_index("ang")]).astype(jnp.int32)
    smem = pl.BlockSpec(memory_space=pltpu.SMEM)
    full = pl.BlockSpec(memory_space=pltpu.VMEM)

    kept, scratch = [], []
    for l in range(SPREAD):
        rows, cols = height >> l, (breadth >> l) + LANES
        kept += [f32(rows + 2 * UP, cols)] * 2
        rows += 2 * (halo >> l)
        scratch += [vmem(rows + 2 * PAD, cols), vmem(rows, cols), vmem(5 * rows, LANES), vmem(rows, cols)]
    piece = (height >> SPREAD, breadth >> SPREAD)
    *kept, coarse = pl.pallas_call(
        lambda *refs: down_kernel(height, total, spacings, *refs),
        out_shape=kept + [f32(*piece)],
        in_specs=[smem] + [full] * 6,
        out_specs=[full] * (2 * SPREAD + 1),
        scratch_shapes=scratch,
        compiler_params=pltpu.CompilerParams(vmem_limit_bytes=50 * 1024 * 1024),
        name="down",
    )(place, guess, halo_v, right_side, halo_g, above, below)

    gathered = lax.all_gather(coarse, ("rad", "ang"), axis=0, tiled=False)
    scratch = []
    for l in range(SPREAD, LEVELS):
        rows, cols = total >> l, max(LANES, (breadth * angs) >> l)
        scratch += [vmem(rows + 2 * PAD, cols), vmem(rows, cols), vmem(5 * rows, LANES), vmem(rows, cols)]
    for l in range(SPREAD):
        rows, cols = (height >> l) + 2 * UP, (breadth >> l) + LANES
        scratch += [vmem(rows + 2 * PAD, cols), vmem(5 * rows, LANES)]
    scratch.append(vmem(height + 2 * UP, breadth + LANES))
    return tuple(
        pl.pallas_call(
            lambda *refs: up_kernel(height, total, spacings, (rads, angs), *refs),
            out_shape=[f32(height, breadth)] * 2,
            in_specs=[smem] + [full] * (2 * SPREAD + 1),
            out_specs=[full] * 2,
            scratch_shapes=scratch,
            compiler_params=pltpu.CompilerParams(vmem_limit_bytes=50 * 1024 * 1024),
            name="up",
        )(place, gathered, *kept)
    )


def solution(mesh):
    placed = (P("rad", "ang"), P("rad", "ang"))
    return jax.shard_map(
        local,
        mesh=mesh,
        in_specs=placed,
        out_specs=(P("rad", "ang"), P("rad", "ang")),
        check_vma=False,
    )
```

time: 618 us -> 127 us (0.21)
  the two profiles are of different devices: /device:TPU:1 before, /device:TPU:0 now
where the time goes in v1:
time: 127 us
  blocking collectives  69.4 us (55%)
  Pallas kernels  38.6 us (30%)
  waiting for transfers between devices  6.69 us (5%)
  starting transfers between devices  6.65 us (5%)
  local copies, waits for them, and re-layouts  3.47 us (3%)
  other arithmetic  1.48 us (1%)
    all_gather x1, blocking collectives, local(): gathered = lax.all_gather(coarse, ('rad', 'ang'), axis=0, tiled=False)  69.4 us
    pallas_call x1, Pallas kernels, local(): pl.pallas_call(lambda *refs: up_kernel(height, total, spacings, (rads, an...  22.3 us
    pallas_call x1, Pallas kernels, local(): pl.pallas_call(lambda *refs: down_kernel(height, total, spacings, *refs),...  16.3 us
    ppermute x1, waiting for transfers between devices, local(): below = lax.ppermute(edge(slice(0, halo)), 'rad', down)  4.31 us
    ppermute x1, starting transfers between devices, local(): before = lax.ppermute(last, 'ang', up)  3.02 us
  transfers between devices with their start and end apart: 4, of which 3 were waited for; matrix products, arithmetic and copies ran while one was open for 2% of the time, Pallas kernels for 0%

profile of v1, /device:TPU:0, one launch (start us, length us, event | category | flops | bytes accessed | tf_op | source)
XLA Modules:
  0.0 127.0 jit_solution(17799372705475185582)
XLA Ops:
  0.6 0.0 copy-start
  0.6 1.1 fusion.6
  1.7 0.1 pad_maximum_fusion.1
  1.8 3.0 %collective-permute-start.1 = (f32[128,128]{1,0:T(8,128)S(1)}, f32[128,128]{1,0:T(8,128)S(1)}, u32[]{:S(2)}, u32[]{:S(2)}) collective-permute-start(f32[128,128]{1,0:T(8,128)S(1)} %pad_maximum_fusion.1), channel_id=1, source_target_pairs={{0,8},{8,16},{16,24},{24,0},{1,9},{9,17},{17,25},{25,1},{2,10},{10... | collective-permute-start | bytes 196616 | tf_op jit(solution)/shard_map/ppermute | solution.py:331
  4.8 0.1 pad_maximum_fusion
  4.9 1.0 collective-permute-start
  6.0 0.0 copy-done
  6.0 1.1 fusion.4
  7.1 0.9 collective-permute-done.1
  8.0 0.1 fusion.9
  8.1 1.4 %collective-permute-done = f32[128,128]{1,0:T(8,128)S(1)} collective-permute-done((f32[128,128]{1,0:T(8,128)S(1)}, f32[128,128]{1,0:T(8,128)S(1)}, u32[]{:S(2)}, u32[]{:S(2)}) %collective-permute-start) | collective-permute-done | bytes 65568 | tf_op jit(solution)/shard_map/ppermute | solution.py:330
  9.6 0.1 fusion.8
  9.6 0.1 fusion.1
  9.7 0.1 fusion.3
  9.9 1.3 %collective-permute-start.2 = (f32[128,1152]{1,0:T(8,128)S(1)}, f32[128,1152]{1,0:T(8,128)S(1)}, u32[]{:S(2)}, u32[]{:S(2)}) collective-permute-start(f32[128,1152]{1,0:T(8,128)S(1)} %maximum_maximum_fusion), channel_id=1, source_target_pairs={{0,1},{1,2},{2,3},{3,4},{4,5},{5,6},{6,7},{8,9},{9,10},{10,11},{11... | collective-permute-start | bytes 1769480 | tf_op jit(solution)/shard_map/ppermute | solution.py:342
  11.2 0.0 copy-start.1
  11.2 0.9 maximum_maximum_fusion.1
  12.1 1.3 %collective-permute-start.3 = (f32[128,1152]{1,0:T(8,128)}, f32[128,1152]{1,0:T(8,128)S(1)}, u32[]{:S(2)}, u32[]{:S(2)}) collective-permute-start(f32[128,1152]{1,0:T(8,128)} %maximum_maximum_fusion.1), channel_id=1, source_target_pairs={{1,0},{2,1},{3,2},{4,3},{5,4},{6,5},{7,6},{9,8},{10,9},{11,10},{12... | collective-permute-start | bytes 1769480 | tf_op jit(solution)/shard_map/ppermute | solution.py:343
  13.4 0.1 pad_add_fusion.refs_0_
  13.4 0.1 pad_maximum_fusion.3.refs_4_
  13.5 0.1 pad_maximum_fusion.2.refs_2_
  13.6 0.0 collective-permute-done.2.refs_5_
  13.6 4.3 %collective-permute-done.3.refs_6_ = f32[128,1152]{1,0:T(8,128)S(1)} collective-permute-done((f32[128,1152]{1,0:T(8,128)}, f32[128,1152]{1,0:T(8,128)S(1)}, u32[]{:S(2)}, u32[]{:S(2)}) %collective-permute-start.3) | collective-permute-done | bytes 589856 | tf_op jit(solution)/shard_map/ppermute | solution.py:343
  17.9 0.0 copy-done.1
  17.9 16.3 %down.1 = (f32[144,1152]{1,0:T(8,128)S(1)}, f32[144,1152]{1,0:T(8,128)}, f32[80,640]{1,0:T(8,128)S(1)}, f32[80,640]{1,0:T(8,128)S(1)}, f32[48,384]{1,0:T(8,128)S...) custom-call(s32[2]{0:T(128)S(1)} %pad_add_fusion.refs_0_, f32[128,1024]{1,0:T(8,128)S(1)} %copy-done, ...), custom_call_target="tpu_custom_call" | custom-call | tf_op jit(solution)/shard_map/down/pallas_call | solution.py:355
  34.3 69.4 %all-gather = f32[512,128]{1,0:T(8,128)S(1)} all-gather(f32[16,128]{1,0:T(8,128)S(1)} %get-tuple-element.9), channel_id=2, replica_groups=mesh['ang'=4,'rad'=8] {'rad','ang'}, dimensions={0}, use_global_device_ids=true | all-gather | bytes 270336 | tf_op jit(solution)/shard_map/all_gather | solution.py:365
  103.7 0.0 copy-start.2
  103.7 1.1 copy-done.2
  104.8 22.3 %up.1 = (f32[128,1024]{1,0:T(8,128)}, f32[128,1024]{1,0:T(8,128)}) custom-call(s32[2]{0:T(128)S(1)} %pad_add_fusion.refs_0_, f32[32,16,128]{2,1,0:T(8,128)S(1)} %bitcast.3, f32[144,1152]{1,0:T(8,128)S(1)} %get-tuple-element.10.refs_2_, f32[144,1152]{1,0:T(8,128)S(1)} %copy-done.2, f32[80,640]{1,0:T(8,128)S(1)} %get-tuple-element.12.refs_4_, ...), custom_call_target="tpu_custom_call" | custom-call | tf_op jit(solution)/shard_map/up/pallas_call | solution.py:375
  (1 shorter events, 0.0 us)
Async XLA Ops:
  0.6 5.3 %copy-start = (f32[128,1024]{1,0:T(8,128)S(1)}, f32[128,1024]{1,0:T(8,128)}, u32[]{:S(2)}) copy-start(f32[128,1024]{1,0:T(8,128)} %refs_1_.1) | copy-start | bytes 1572868
  1.8 6.2 %collective-permute-start.1 = (f32[128,128]{1,0:T(8,128)S(1)}, f32[128,128]{1,0:T(8,128)S(1)}, u32[]{:S(2)}, u32[]{:S(2)}) collective-permute-start(f32[128,128]{1,0:T(8,128)S(1)} %pad_maximum_fusion.1), channel_id=1, source_target_pairs={{0,8},{8,16},{16,24},{24,0},{1,9},{9,17},{17,25},{25,1},{2,10},{10... | collective-permute-start | bytes 196616 | tf_op jit(solution)/shard_map/ppermute | solution.py:331
  4.9 4.6 %collective-permute-start = (f32[128,128]{1,0:T(8,128)S(1)}, f32[128,128]{1,0:T(8,128)S(1)}, u32[]{:S(2)}, u32[]{:S(2)}) collective-permute-start(f32[128,128]{1,0:T(8,128)S(1)} %pad_maximum_fusion), channel_id=1, source_target_pairs={{8,0},{16,8},{24,16},{0,24},{9,1},{17,9},{25,17},{1,25},{10,2},{18... | collective-permute-start | bytes 196616 | tf_op jit(solution)/shard_map/ppermute | solution.py:330
  9.9 3.8 %collective-permute-start.2 = (f32[128,1152]{1,0:T(8,128)S(1)}, f32[128,1152]{1,0:T(8,128)S(1)}, u32[]{:S(2)}, u32[]{:S(2)}) collective-permute-start(f32[128,1152]{1,0:T(8,128)S(1)} %maximum_maximum_fusion), channel_id=1, source_target_pairs={{0,1},{1,2},{2,3},{3,4},{4,5},{5,6},{6,7},{8,9},{9,10},{10,11},{11... | collective-permute-start | bytes 1769480 | tf_op jit(solution)/shard_map/ppermute | solution.py:342
  11.2 6.7 %copy-start.1 = (f32[128,1024]{1,0:T(8,128)S(1)}, f32[128,1024]{1,0:T(8,128)}, u32[]{:S(2)}) copy-start(f32[128,1024]{1,0:T(8,128)} %refs_3_.1) | copy-start | bytes 1572868
  12.1 5.9 %collective-permute-start.3 = (f32[128,1152]{1,0:T(8,128)}, f32[128,1152]{1,0:T(8,128)S(1)}, u32[]{:S(2)}, u32[]{:S(2)}) collective-permute-start(f32[128,1152]{1,0:T(8,128)} %maximum_maximum_fusion.1), channel_id=1, source_target_pairs={{1,0},{2,1},{3,2},{4,3},{5,4},{6,5},{7,6},{9,8},{10,9},{11,10},{12... | collective-permute-start | bytes 1769480 | tf_op jit(solution)/shard_map/ppermute | solution.py:343
  103.7 1.1 copy-start.2

commit v2 on v1

--- a/solution.py
+++ b/solution.py
@@ -213,7 +213,7 @@
     return dot(weights, p)
 
 
-def down_kernel(height, total, spacings, place, v, hv, g, hg, top, bottom, *refs):
+def down_kernel(height, total, spacings, place, v, hv, g, hg, top, bottom, htop, hbottom, *refs):
     outs, scratch = refs[: 2 * SPREAD + 1], refs[2 * SPREAD + 1 :]
     halo = UP << SPREAD
     breadth = v.shape[1]
@@ -222,13 +222,14 @@
     at = pl.ds(PAD + halo, height)
     vb[at, pl.ds(0, breadth)] = v[...]
     vb[at, pl.ds(breadth, LANES)] = hv[...]
-    vb[pl.ds(PAD, halo), :] = top[pl.ds(0, halo), :]
-    vb[pl.ds(PAD + halo + height, halo), :] = bottom[pl.ds(0, halo), :]
+    for buf, take, shift in ((vb, 0, PAD), (gb, halo, 0)):
+        for at, block, corner in ((0, top, htop), (halo + height, bottom, hbottom)):
+            at = pl.ds(at + shift, halo)
+            buf[at, pl.ds(0, breadth)] = block[pl.ds(take, halo), :]
+            buf[at, pl.ds(breadth, LANES)] = corner[pl.ds(take, halo), :]
     at = pl.ds(halo, height)
     gb[at, pl.ds(0, breadth)] = g[...]
     gb[at, pl.ds(breadth, LANES)] = hg[...]
-    gb[pl.ds(0, halo), :] = top[pl.ds(halo, halo), :]
-    gb[pl.ds(halo + height, halo), :] = bottom[pl.ds(halo, halo), :]
     for l in range(SPREAD):
         vb, gb, cf, s = scratch[4 * l : 4 * l + 4]
         edge = halo >> l
@@ -260,9 +261,10 @@
         whole.append((Level(v, g, cf, spacings[l], total >> l, 0), s))
     g = whole[0][0].g
     piece = gathered.shape[1:]
-    for r in range(rads):
-        for a in range(angs):
-            g[pl.ds(r * piece[0], piece[0]), pl.ds(a * piece[1], piece[1])] = gathered[r * angs + a]
+    for k, (r, a) in enumerate(gather_order(rads, angs)[1]):
+        row = pl.multiple_of((place[0] ^ r) * piece[0], 8)
+        col = pl.multiple_of((place[1] ^ a) * piece[1], LANES)
+        g[pl.ds(row, piece[0]), pl.ds(col, piece[1])] = gathered[k]
 
     def period(l):
         return (piece[1] * angs) >> (l - SPREAD)
@@ -309,6 +311,24 @@
     out_s[...] = s[pl.ds(UP, height), pl.ds(0, breadth)]
 
 
+def gather_order(rads, angs):
+    rounds = [("rad", 1 << k) for k in range(rads.bit_length() - 2, 0, -1)]
+    rounds += [("ang", 1 << k) for k in range(angs.bit_length() - 1)]
+    rounds += [("rad", 1)] if rads > 1 else []
+    held = [(0, 0)]
+    for axis, bit in rounds:
+        held += [(r ^ bit, a) if axis == "rad" else (r, a ^ bit) for r, a in held]
+    return rounds, held
+
+
+def gather_pieces(piece, rads, angs):
+    held = piece[None]
+    for axis, bit in gather_order(rads, angs)[0]:
+        pairs = [(i, i ^ bit) for i in range(lax.axis_size(axis))]
+        held = jnp.concatenate([held, lax.ppermute(held, axis, pairs)], axis=0)
+    return held
+
+
 def f32(*shape):
     return jax.ShapeDtypeStruct(shape, jnp.float32)
 
@@ -323,24 +343,24 @@
     total = height * rads
     spacings = [2.0 * math.pi / ((breadth * angs) >> l) for l in range(LEVELS)]
     halo = UP << SPREAD
-    up = [(i, (i + 1) % angs) for i in range(angs)]
+    ring_up = [(i, (i + 1) % angs) for i in range(angs)]
+    ring_down = [(j, i) for i, j in ring_up]
+    up = [(i, i + 1) for i in range(rads - 1)]
     down = [(j, i) for i, j in up]
+
+    def spread(x, y):
+        last = jnp.concatenate([x[-halo:], y[-halo:]], axis=0)
+        leading = jnp.concatenate([x[:halo], y[:halo]], axis=0)
+        return lax.ppermute(last, "rad", up), lax.ppermute(leading, "rad", down)
+
+    above, below = spread(guess, right_side)
     first = jnp.concatenate([guess[:, :SIDE], right_side[:, :SIDE]], axis=1)
     last = jnp.concatenate([guess[:, -SIDE:], right_side[:, -SIDE:]], axis=1)
-    after = lax.ppermute(first, "ang", down)
-    before = lax.ppermute(last, "ang", up)
+    after = lax.ppermute(first, "ang", ring_down)
+    before = lax.ppermute(last, "ang", ring_up)
     halo_v = jnp.concatenate([after[:, :SIDE], before[:, :SIDE]], axis=1)
     halo_g = jnp.concatenate([after[:, SIDE:], before[:, SIDE:]], axis=1)
-
-    def edge(at):
-        top = jnp.concatenate([guess[at], halo_v[at]], axis=1)
-        low = jnp.concatenate([right_side[at], halo_g[at]], axis=1)
-        return jnp.concatenate([top, low], axis=0)
-
-    up = [(i, i + 1) for i in range(rads - 1)]
-    down = [(j, i) for i, j in up]
-    above = lax.ppermute(edge(slice(-halo, None)), "rad", up)
-    below = lax.ppermute(edge(slice(0, halo)), "rad", down)
+    corner_above, corner_below = spread(halo_v, halo_g)
     place = jnp.stack([lax.axis_index("rad"), lax.axis_index("ang")]).astype(jnp.int32)
     smem = pl.BlockSpec(memory_space=pltpu.SMEM)
     full = pl.BlockSpec(memory_space=pltpu.VMEM)
@@ -355,14 +375,14 @@
     *kept, coarse = pl.pallas_call(
         lambda *refs: down_kernel(height, total, spacings, *refs),
         out_shape=kept + [f32(*piece)],
-        in_specs=[smem] + [full] * 6,
+        in_specs=[smem] + [full] * 8,
         out_specs=[full] * (2 * SPREAD + 1),
         scratch_shapes=scratch,
         compiler_params=pltpu.CompilerParams(vmem_limit_bytes=50 * 1024 * 1024),
         name="down",
-    )(place, guess, halo_v, right_side, halo_g, above, below)
-
-    gathered = lax.all_gather(coarse, ("rad", "ang"), axis=0, tiled=False)
+    )(place, guess, halo_v, right_side, halo_g, above, below, corner_above, corner_below)
+
+    gathered = gather_pieces(coarse, rads, angs)
     scratch = []
     for l in range(SPREAD, LEVELS):
         rows, cols = total >> l, max(LANES, (breadth * angs) >> l)

time: 127 us -> 77.8 us (0.61)
  blocking collectives: 69.4 us -> 0 us
  starting transfers between devices: 6.65 us -> 21.1 us
  waiting for transfers between devices: 6.69 us -> 13.9 us
    all_gather x1 -> x0, blocking collectives: 69.4 us -> none  [local(): gathered = lax.all_gather(coarse, ('rad', 'ang'), axis=0, tiled=False)]
    ppermute x4 -> x11, starting transfers between devices: 6.65 us -> 21.1 us  [the longest x4 9.18 us: spread(): return (lax.ppermute(last, 'rad', up), lax.ppermute(leading, 'rad', down))]
    ppermute x4 -> x11, waiting for transfers between devices: 6.69 us -> 13.9 us  [the longest x5 11 us: gather_pieces(): held = jnp.concatenate([held, lax.ppermute(held, axis, pairs)], axis=0)]
  transfers between devices with their start and end apart: 4 -> 11, of which waited for: 3 -> 6; matrix products, arithmetic and copies ran while one was open for 2% -> 2% of each run, Pallas kernels for 0% -> 0%
where the time goes in v2:
time: 77.8 us; the launch traced here: 77.5 us
  Pallas kernels  38.6 us (50%)
  starting transfers between devices  21.1 us (27%)
  waiting for transfers between devices  13.9 us (18%)
  local copies, waits for them, and re-layouts  2.42 us (3%)
  between operations  0.83 us (1%)
    pallas_call x1, Pallas kernels, local(): pl.pallas_call(lambda *refs: up_kernel(height, total, spacings, (rads, an...  22.3 us
    pallas_call x1, Pallas kernels, local(): pl.pallas_call(lambda *refs: down_kernel(height, total, spacings, *refs),...  16.4 us
    ppermute x5, waiting for transfers between devices, gather_pieces(): held = jnp.concatenate([held, lax.ppermute(held, axis, pairs)], axis=0)  11 us
    ppermute x4, starting transfers between devices, spread(): return (lax.ppermute(last, 'rad', up), lax.ppermute(leading, 'rad', down))  9.18 us
    ppermute x5, starting transfers between devices, gather_pieces(): held = jnp.concatenate([held, lax.ppermute(held, axis, pairs)], axis=0)  7.88 us
    ppermute x1, starting transfers between devices, local(): before = lax.ppermute(last, 'ang', ring_up)  3.02 us
    ppermute x4, waiting for transfers between devices, spread(): return (lax.ppermute(last, 'rad', up), lax.ppermute(leading, 'rad', down))  2.9 us
  transfers between devices with their start and end apart: 11, of which 6 were waited for; matrix products, arithmetic and copies ran while one was open for 2% of the time, Pallas kernels for 0%

profile of v2, /device:TPU:0, one launch (start us, length us, event | category | flops | bytes accessed | tf_op | source)
XLA Modules:
  0.0 77.5 jit_solution(5118558413886288552)
XLA Ops:
  0.6 0.0 copy-start
  0.6 1.1 %fusion.6 = (f32[128,64]{1,0:T(8,128)S(1)}, f32[128,64]{1,0:T(8,128)S(1)}, f32[128,64]{1,0:T(8,128)S(1)}, f32[128,64]{1,0:T(8,128)S(1)}) fusion(f32[128,1024]{1,0:T(8,128)} %refs_1_.1, f32[128,1024]{1,0:T(8,128)} %refs_3_.1), kind=kLoop, calls=%fused_computation.37 | loop fusion | bytes 262144 | tf_op jit(solution)/shard_map/slice | solution.py:357
  1.7 0.1 pad_maximum_fusion.3
  1.8 3.0 %collective-permute-start.1 = (f32[128,128]{1,0:T(8,128)S(1)}, f32[128,128]{1,0:T(8,128)S(1)}, u32[]{:S(2)}, u32[]{:S(2)}) collective-permute-start(f32[128,128]{1,0:T(8,128)S(1)} %pad_maximum_fusion.3), channel_id=1, source_target_pairs={{0,8},{8,16},{16,24},{24,0},{1,9},{9,17},{17,25},{25,1},{2,10},{10... | collective-permute-start | bytes 196616 | tf_op jit(solution)/shard_map/ppermute | solution.py:360
  4.8 0.1 pad_maximum_fusion.2
  4.9 1.0 %collective-permute-start = (f32[128,128]{1,0:T(8,128)S(1)}, f32[128,128]{1,0:T(8,128)S(1)}, u32[]{:S(2)}, u32[]{:S(2)}) collective-permute-start(f32[128,128]{1,0:T(8,128)S(1)} %pad_maximum_fusion.2), channel_id=1, source_target_pairs={{8,0},{16,8},{24,16},{0,24},{9,1},{17,9},{25,17},{1,25},{10,2},{18... | collective-permute-start | bytes 196616 | tf_op jit(solution)/shard_map/ppermute | solution.py:359
  6.0 0.0 copy-done
  6.0 1.1 %fusion.4 = (f32[64,1024]{1,0:T(8,128)S(1)}, f32[64,1024]{1,0:T(8,128)S(1)}, f32[64,1024]{1,0:T(8,128)S(1)}, f32[64,1024]{1,0:T(8,128)S(1)}) fusion(f32[128,1024]{1,0:T(8,128)S(1)} %copy-done, f32[128,1024]{1,0:T(8,128)} %refs_3_.1), kind=kLoop, calls=%fused_computation.35 | loop fusion | bytes 2097152 | tf_op jit(solution)/shard_map/slice | solution.py:353
  7.1 1.5 %collective-permute-start.2 = (f32[128,1024]{1,0:T(8,128)S(1)}, f32[128,1024]{1,0:T(8,128)S(1)}, u32[]{:S(2)}, u32[]{:S(2)}) collective-permute-start(f32[128,1024]{1,0:T(8,128)S(1)} %pad_maximum_fusion), channel_id=1, source_target_pairs={{0,1},{1,2},{2,3},{3,4},{4,5},{5,6},{6,7},{8,9},{9,10},{10,11},{11... | collective-permute-start | bytes 1572872 | tf_op jit(solution)/shard_map/ppermute | solution.py:354
  8.7 1.3 %collective-permute-start.3 = (f32[128,1024]{1,0:T(8,128)S(1)}, f32[128,1024]{1,0:T(8,128)S(1)}, u32[]{:S(2)}, u32[]{:S(2)}) collective-permute-start(f32[128,1024]{1,0:T(8,128)S(1)} %pad_maximum_fusion.1), channel_id=1, source_target_pairs={{1,0},{2,1},{3,2},{4,3},{5,4},{6,5},{7,6},{9,8},{10,9},{11,10},{12... | collective-permute-start | bytes 1572872 | tf_op jit(solution)/shard_map/ppermute | solution.py:354
  10.0 0.1 pad_add_fusion.refs_0_
  10.1 0.0 collective-permute-done.1
  10.1 0.1 fusion.9
  10.2 0.0 collective-permute-done
  10.2 0.1 fusion.8
  10.2 0.0 copy-start.1
  10.2 0.1 fusion.1
  10.3 0.1 fusion.3
  10.5 5.1 %collective-permute-start.4 = (f32[128,128]{1,0:T(8,128)S(1)}, f32[128,128]{1,0:T(8,128)S(1)}, u32[]{:S(2)}, u32[]{:S(2)}) collective-permute-start(f32[128,128]{1,0:T(8,128)S(1)} %pad_maximum_fusion.4), channel_id=1, source_target_pairs={{0,1},{1,2},{2,3},{3,4},{4,5},{5,6},{6,7},{8,9},{9,10},{10,11},{11... | collective-permute-start | bytes 196616 | tf_op jit(solution)/shard_map/ppermute | solution.py:354
  15.6 1.3 %collective-permute-start.5 = (f32[128,128]{1,0:T(8,128)S(1)}, f32[128,128]{1,0:T(8,128)S(1)}, u32[]{:S(2)}, u32[]{:S(2)}) collective-permute-start(f32[128,128]{1,0:T(8,128)S(1)} %pad_maximum_fusion.5), channel_id=1, source_target_pairs={{1,0},{2,1},{3,2},{4,3},{5,4},{6,5},{7,6},{9,8},{10,9},{11,10},{12... | collective-permute-start | bytes 196616 | tf_op jit(solution)/shard_map/ppermute | solution.py:354
  16.9 0.1 pad_maximum_fusion.8.refs_4_
  17.0 0.1 pad_maximum_fusion.7.refs_2_
  17.1 0.0 collective-permute-done.4.refs_7_
  17.1 2.9 %collective-permute-done.5.refs_8_ = f32[128,128]{1,0:T(8,128)S(1)} collective-permute-done((f32[128,128]{1,0:T(8,128)S(1)}, f32[128,128]{1,0:T(8,128)S(1)}, u32[]{:S(2)}, u32[]{:S(2)}) %collective-permute-start.5) | collective-permute-done | bytes 65568 | tf_op jit(solution)/shard_map/ppermute | solution.py:354
  20.0 0.0 collective-permute-done.2.refs_5_
  20.0 0.0 collective-permute-done.3.refs_6_
  20.0 0.0 copy-done.1
  20.0 16.4 %down.1 = (f32[144,1152]{1,0:T(8,128)S(1)}, f32[144,1152]{1,0:T(8,128)}, f32[80,640]{1,0:T(8,128)S(1)}, f32[80,640]{1,0:T(8,128)S(1)}, f32[48,384]{1,0:T(8,128)S...) custom-call(s32[2]{0:T(128)S(1)} %pad_add_fusion.refs_0_, f32[128,1024]{1,0:T(8,128)S(1)} %copy-done, ...), custom_call_target="tpu_custom_call" | custom-call | tf_op jit(solution)/shard_map/down/pallas_call | solution.py:375
  36.3 0.0 copy-start.2
  36.3 3.8 %collective-permute-start.6 = (f32[1,16,128]{2,1,0:T(8,128)S(1)}, f32[1,16,128]{2,1,0:T(8,128)S(1)}, u32[]{:S(2)}, u32[]{:S(2)}) collective-permute-start(f32[1,16,128]{2,1,0:T(8,128)S(1)} %bitcast.5), channel_id=1, source_target_pairs={{0,4},{1,5},{2,6},{3,7},{4,0},{5,1},{6,2},{7,3},{8,12},{9,13},{10,... | collective-permute-start | bytes 24584 | tf_op jit(solution)/shard_map/ppermute | solution.py:328
  40.1 1.6 %collective-permute-done.6 = f32[1,16,128]{2,1,0:T(8,128)S(1)} collective-permute-done((f32[1,16,128]{2,1,0:T(8,128)S(1)}, f32[1,16,128]{2,1,0:T(8,128)S(1)}, u32[]{:S(2)}, u32[]{:S(2)}) %collective-permute-start.6) | collective-permute-done | bytes 8224 | tf_op jit(solution)/shard_map/ppermute | solution.py:328
  41.8 1.9 %collective-permute-start.7 = (f32[2,16,128]{2,1,0:T(8,128)S(1)}, f32[2,16,128]{2,1,0:T(8,128)S(1)}, u32[]{:S(2)}, u32[]{:S(2)}) collective-permute-start(f32[2,16,128]{2,1,0:T(8,128)S(1)} %pad_maximum_fusion.10), channel_id=1, source_target_pairs={{0,2},{1,3},{2,0},{3,1},{4,6},{5,7},{6,4},{7,5},{8,10},{9,11},{10,... | collective-permute-start | bytes 49160 | tf_op jit(solution)/shard_map/ppermute | solution.py:328
  43.7 1.9 %collective-permute-done.7 = f32[2,16,128]{2,1,0:T(8,128)S(1)} collective-permute-done((f32[2,16,128]{2,1,0:T(8,128)S(1)}, f32[2,16,128]{2,1,0:T(8,128)S(1)}, u32[]{:S(2)}, u32[]{:S(2)}) %collective-permute-start.7) | collective-permute-done | bytes 16416 | tf_op jit(solution)/shard_map/ppermute | solution.py:328
  45.6 0.6 collective-permute-start.8
  46.2 3.3 %collective-permute-done.8 = f32[4,16,128]{2,1,0:T(8,128)S(1)} collective-permute-done((f32[4,16,128]{2,1,0:T(8,128)S(1)}, f32[4,16,128]{2,1,0:T(8,128)S(1)}, u32[]{:S(2)}, u32[]{:S(2)}) %collective-permute-start.8) | collective-permute-done | bytes 32800 | tf_op jit(solution)/shard_map/ppermute | solution.py:328
  49.5 1.5 %collective-permute-start.9 = (f32[8,16,128]{2,1,0:T(8,128)S(1)}, f32[8,16,128]{2,1,0:T(8,128)S(1)}, u32[]{:S(2)}, u32[]{:S(2)}) collective-permute-start(f32[8,16,128]{2,1,0:T(8,128)S(1)} %pad_maximum_fusion.6), channel_id=1, source_target_pairs={{0,16},{8,24},{16,0},{24,8},{1,17},{9,25},{17,1},{25,9},{2,18},{10... | collective-permute-start | bytes 196616 | tf_op jit(solution)/shard_map/ppermute | solution.py:328
  51.1 2.7 %collective-permute-done.9 = f32[8,16,128]{2,1,0:T(8,128)S(1)} collective-permute-done((f32[8,16,128]{2,1,0:T(8,128)S(1)}, f32[8,16,128]{2,1,0:T(8,128)S(1)}, u32[]{:S(2)}, u32[]{:S(2)}) %collective-permute-start.9) | collective-permute-done | bytes 65568 | tf_op jit(solution)/shard_map/ppermute | solution.py:328
  53.8 0.1 collective-permute-start.10
  53.9 1.3 %collective-permute-done.10 = f32[16,16,128]{2,1,0:T(8,128)S(1)} collective-permute-done((f32[16,16,128]{2,1,0:T(8,128)S(1)}, f32[16,16,128]{2,1,0:T(8,128)S(1)}, u32[]{:S(2)}, u32[]{:S(2)}) %collective-permute-start.10) | collective-permute-done | bytes 131104 | tf_op jit(solution)/shard_map/ppermute | solution.py:328
  55.3 0.0 copy-done.2
  55.3 22.3 %up.1 = (f32[128,1024]{1,0:T(8,128)}, f32[128,1024]{1,0:T(8,128)}) custom-call(s32[2]{0:T(128)S(1)} %pad_add_fusion.refs_0_, f32[32,16,128]{2,1,0:T(8,128)S(1)} %constant_dynamic-update-slice_fusion.5.refs_1_, f32[144,1152]{1,0:T(8,128)S(1)} %get-tuple-element.10.refs_2_, f32[144,1152]{1,0:T(8,128)S(1)} %copy-done.2, ...), custom_call_target="tpu_custom_call" | custom-call | tf_op jit(solution)/shard_map/up/pallas_call | solution.py:395
  (13 shorter events, 0.1 us)
Async XLA Ops:
  0.6 5.3 %copy-start = (f32[128,1024]{1,0:T(8,128)S(1)}, f32[128,1024]{1,0:T(8,128)}, u32[]{:S(2)}) copy-start(f32[128,1024]{1,0:T(8,128)} %refs_1_.1) | copy-start | bytes 1572868
  1.8 8.2 %collective-permute-start.1 = (f32[128,128]{1,0:T(8,128)S(1)}, f32[128,128]{1,0:T(8,128)S(1)}, u32[]{:S(2)}, u32[]{:S(2)}) collective-permute-start(f32[128,128]{1,0:T(8,128)S(1)} %pad_maximum_fusion.3), channel_id=1, source_target_pairs={{0,8},{8,16},{16,24},{24,0},{1,9},{9,17},{17,25},{25,1},{2,10},{10... | collective-permute-start | bytes 196616 | tf_op jit(solution)/shard_map/ppermute | solution.py:360
  4.9 5.2 %collective-permute-start = (f32[128,128]{1,0:T(8,128)S(1)}, f32[128,128]{1,0:T(8,128)S(1)}, u32[]{:S(2)}, u32[]{:S(2)}) collective-permute-start(f32[128,128]{1,0:T(8,128)S(1)} %pad_maximum_fusion.2), channel_id=1, source_target_pairs={{8,0},{16,8},{24,16},{0,24},{9,1},{17,9},{25,17},{1,25},{10,2},{18... | collective-permute-start | bytes 196616 | tf_op jit(solution)/shard_map/ppermute | solution.py:359
  7.1 12.8 %collective-permute-start.2 = (f32[128,1024]{1,0:T(8,128)S(1)}, f32[128,1024]{1,0:T(8,128)S(1)}, u32[]{:S(2)}, u32[]{:S(2)}) collective-permute-start(f32[128,1024]{1,0:T(8,128)S(1)} %pad_maximum_fusion), channel_id=1, source_target_pairs={{0,1},{1,2},{2,3},{3,4},{4,5},{5,6},{6,7},{8,9},{9,10},{10,11},{11... | collective-permute-start | bytes 1572872 | tf_op jit(solution)/shard_map/ppermute | solution.py:354
  8.7 11.3 %collective-permute-start.3 = (f32[128,1024]{1,0:T(8,128)S(1)}, f32[128,1024]{1,0:T(8,128)S(1)}, u32[]{:S(2)}, u32[]{:S(2)}) collective-permute-start(f32[128,1024]{1,0:T(8,128)S(1)} %pad_maximum_fusion.1), channel_id=1, source_target_pairs={{1,0},{2,1},{3,2},{4,3},{5,4},{6,5},{7,6},{9,8},{10,9},{11,10},{12... | collective-permute-start | bytes 1572872 | tf_op jit(solution)/shard_map/ppermute | solution.py:354
  10.2 9.7 %copy-start.1 = (f32[128,1024]{1,0:T(8,128)S(1)}, f32[128,1024]{1,0:T(8,128)}, u32[]{:S(2)}) copy-start(f32[128,1024]{1,0:T(8,128)} %refs_3_.1) | copy-start | bytes 1572868
  10.5 6.6 %collective-permute-start.4 = (f32[128,128]{1,0:T(8,128)S(1)}, f32[128,128]{1,0:T(8,128)S(1)}, u32[]{:S(2)}, u32[]{:S(2)}) collective-permute-start(f32[128,128]{1,0:T(8,128)S(1)} %pad_maximum_fusion.4), channel_id=1, source_target_pairs={{0,1},{1,2},{2,3},{3,4},{4,5},{5,6},{6,7},{8,9},{9,10},{10,11},{11... | collective-permute-start | bytes 196616 | tf_op jit(solution)/shard_map/ppermute | solution.py:354
  15.6 4.4 %collective-permute-start.5 = (f32[128,128]{1,0:T(8,128)S(1)}, f32[128,128]{1,0:T(8,128)S(1)}, u32[]{:S(2)}, u32[]{:S(2)}) collective-permute-start(f32[128,128]{1,0:T(8,128)S(1)} %pad_maximum_fusion.5), channel_id=1, source_target_pairs={{1,0},{2,1},{3,2},{4,3},{5,4},{6,5},{7,6},{9,8},{10,9},{11,10},{12... | collective-permute-start | bytes 196616 | tf_op jit(solution)/shard_map/ppermute | solution.py:354
  36.3 18.9 %copy-start.2 = (f32[144,1152]{1,0:T(8,128)S(1)}, f32[144,1152]{1,0:T(8,128)}, u32[]{:S(2)}) copy-start(f32[144,1152]{1,0:T(8,128)} %get-tuple-element.11.refs_3_) | copy-start | bytes 1990660
  36.3 5.4 %collective-permute-start.6 = (f32[1,16,128]{2,1,0:T(8,128)S(1)}, f32[1,16,128]{2,1,0:T(8,128)S(1)}, u32[]{:S(2)}, u32[]{:S(2)}) collective-permute-start(f32[1,16,128]{2,1,0:T(8,128)S(1)} %bitcast.5), channel_id=1, source_target_pairs={{0,4},{1,5},{2,6},{3,7},{4,0},{5,1},{6,2},{7,3},{8,12},{9,13},{10,... | collective-permute-start | bytes 24584 | tf_op jit(solution)/shard_map/ppermute | solution.py:328
  41.8 3.9 %collective-permute-start.7 = (f32[2,16,128]{2,1,0:T(8,128)S(1)}, f32[2,16,128]{2,1,0:T(8,128)S(1)}, u32[]{:S(2)}, u32[]{:S(2)}) collective-permute-start(f32[2,16,128]{2,1,0:T(8,128)S(1)} %pad_maximum_fusion.10), channel_id=1, source_target_pairs={{0,2},{1,3},{2,0},{3,1},{4,6},{5,7},{6,4},{7,5},{8,10},{9,11},{10,... | collective-permute-start | bytes 49160 | tf_op jit(solution)/shard_map/ppermute | solution.py:328
  45.6 3.9 %collective-permute-start.8 = (f32[4,16,128]{2,1,0:T(8,128)S(1)}, f32[4,16,128]{2,1,0:T(8,128)S(1)}, u32[]{:S(2)}, u32[]{:S(2)}) collective-permute-start(f32[4,16,128]{2,1,0:T(8,128)S(1)} %pad_maximum_fusion.9), channel_id=1, source_target_pairs={{0,8},{8,0},{16,24},{24,16},{1,9},{9,1},{17,25},{25,17},{2,10},{10... | collective-permute-start | bytes 98312 | tf_op jit(solution)/shard_map/ppermute | solution.py:328
  49.5 4.3 %collective-permute-start.9 = (f32[8,16,128]{2,1,0:T(8,128)S(1)}, f32[8,16,128]{2,1,0:T(8,128)S(1)}, u32[]{:S(2)}, u32[]{:S(2)}) collective-permute-start(f32[8,16,128]{2,1,0:T(8,128)S(1)} %pad_maximum_fusion.6), channel_id=1, source_target_pairs={{0,16},{8,24},{16,0},{24,8},{1,17},{9,25},{17,1},{25,9},{2,18},{10... | collective-permute-start | bytes 196616 | tf_op jit(solution)/shard_map/ppermute | solution.py:328
  53.8 1.4 %collective-permute-start.10 = (f32[16,16,128]{2,1,0:T(8,128)S(1)}, f32[16,16,128]{2,1,0:T(8,128)S(1)}, u32[]{:S(2)}, u32[]{:S(2)}) collective-permute-start(f32[16,16,128]{2,1,0:T(8,128)S(1)} %get-tuple-element.28), channel_id=1, source_target_pairs={{0,1},{1,0},{2,3},{3,2},{4,5},{5,4},{6,7},{7,6},{8,9},{9,8},{10,11... | collective-permute-start | bytes 393224 | tf_op jit(solution)/shard_map/ppermute | solution.py:328

commit v3 on v2

--- a/solution.py
+++ b/solution.py
@@ -16,17 +16,31 @@
 UP = 8
 LANES = 128
 SIDE = 64
-HIGH = lax.Precision.HIGHEST
 
 
 def iota(shape, dim):
     return lax.broadcasted_iota(jnp.int32, shape, dim)
 
 
-def dot(a, b):
-    return lax.dot_general(
-        a, b, (((1,), (0,)), ((), ())), precision=HIGH, preferred_element_type=jnp.float32
-    )
+def thirds(x):
+    high = x.astype(jnp.bfloat16)
+    rest = x - high.astype(jnp.float32)
+    middle = rest.astype(jnp.bfloat16)
+    return high, middle, (rest - middle.astype(jnp.float32)).astype(jnp.bfloat16)
+
+
+def product(a, b):
+    return lax.dot_general(a, b, (((1,), (0,)), ((), ())), preferred_element_type=jnp.float32)
+
+
+def dot(a, b, exact):
+    if exact == 0:
+        a = a.astype(jnp.bfloat16)
+        high, middle, low = [product(a, x) for x in thirds(b)]
+    else:
+        b = b.astype(jnp.bfloat16)
+        high, middle, low = [product(x, b) for x in thirds(a)]
+    return high + (middle + low)
 
 
 def wide(x, breadth):
@@ -37,7 +51,7 @@
     units = rows // 8
     best = 1
     for n in range(1, units + 1):
-        if units % n == 0 and n * 8 * breadth <= 20 * 1024:
+        if units % n == 0 and n * 8 * breadth <= 80 * 1024:
             best = n
     return 8 * best
 
@@ -148,7 +162,7 @@
         0.375,
         jnp.where(jnp.logical_or(gap == -1, gap == 2), 0.125, 0.0),
     ).astype(jnp.float32)
-    t = dot(weights, s[...])
+    t = dot(weights, s[...], 0)
     u = 0.5 * (
         pltpu.roll(t, 1, 1)
         + 3.0 * t
@@ -161,17 +175,17 @@
         shape = (2 * LANES, LANES)
         pick = one(iota(shape, 0) == 2 * iota(shape, 1))
         for k in range(own // (2 * LANES)):
-            tiles.append(dot(u[:, 2 * LANES * k : 2 * LANES * (k + 1)], pick))
+            tiles.append(dot(u[:, 2 * LANES * k : 2 * LANES * (k + 1)], pick, 1))
     else:
         shape = (LANES, LANES)
         pick = one(iota(shape, 0) == 2 * (iota(shape, 1) % (period // 2)))
-        tiles.append(dot(u, pick))
+        tiles.append(dot(u, pick, 1))
     if halo:
         shape = (LANES, LANES)
         j, i = iota(shape, 0), iota(shape, 1)
         right = jnp.logical_and(j == 2 * i, j < SIDE)
         left = jnp.logical_and(j == 2 * i - LANES, j >= SIDE)
-        tiles.append(dot(u[:, own:], one(jnp.logical_or(right, left))))
+        tiles.append(dot(u[:, own:], one(jnp.logical_or(right, left)), 1))
     return tiles[0] if len(tiles) == 1 else jnp.concatenate(tiles, axis=1)
 
 
@@ -191,26 +205,26 @@
         i, j = iota(shape, 0), iota(shape, 1)
         spread = one(j == jnp.where(i < LANES, 2 * i, 2 * (i - LANES) + 1))
         for k in range(own // LANES):
-            tiles.append(dot(pair(k), spread))
+            tiles.append(dot(pair(k), spread, 1))
     else:
         shape = (2 * LANES, LANES)
         i, j = iota(shape, 0), iota(shape, 1) % fine_period
         spread = one(j == jnp.where(i < LANES, 2 * i, 2 * (i - LANES) + 1))
-        tiles.append(dot(pair(0), spread))
+        tiles.append(dot(pair(0), spread, 1))
     if halo:
         shape = (2 * LANES, LANES)
         i, j = iota(shape, 0), iota(shape, 1)
         lane = i % LANES
         source = jnp.where(j < SIDE, j // 2, j // 2 + SIDE)
         spread = one(jnp.logical_and(lane == source, i // LANES == j % 2))
-        tiles.append(dot(pair(own // LANES), spread))
+        tiles.append(dot(pair(own // LANES), spread, 1))
     p = tiles[0] if len(tiles) == 1 else jnp.concatenate(tiles, axis=1)
     shape = (rows, e.shape[0])
     i, c = iota(shape, 0), iota(shape, 1)
     near = i // 2 + shift
     far = near + jnp.where(i % 2 == 0, -1, 1)
     weights = jnp.where(c == near, 0.75, jnp.where(c == far, 0.25, 0.0)).astype(jnp.float32)
-    return dot(weights, p)
+    return dot(weights, p, 0)
 
 
 def down_kernel(height, total, spacings, place, v, hv, g, hg, top, bottom, htop, hbottom, *refs):

time: 77.8 us -> 64.8 us (0.83)
  Pallas kernels: 38.6 us -> 25.6 us
    pallas_call x1, Pallas kernels: 22.3 us -> 15.4 us  [local(): pl.pallas_call(lambda *refs: up_kernel(height, total, spacings, (rads, an...]
    pallas_call x1, Pallas kernels: 16.4 us -> 10.3 us  [local(): pl.pallas_call(lambda *refs: down_kernel(height, total, spacings, *refs),...]
  transfers between devices with their start and end apart: 11 -> 11, of which waited for: 6 -> 6; matrix products, arithmetic and copies ran while one was open for 2% -> 3% of each run, Pallas kernels for 0% -> 0%
where the time goes in v3:
time: 64.8 us; the launch traced here: 64.6 us
  Pallas kernels  25.6 us (40%)
  starting transfers between devices  21.1 us (33%)
  waiting for transfers between devices  13.9 us (21%)
  local copies, waits for them, and re-layouts  2.42 us (4%)
  between operations  0.83 us (1%)
  other arithmetic  0.68 us (1%)
    pallas_call x1, Pallas kernels, local(): pl.pallas_call(lambda *refs: up_kernel(height, total, spacings, (rads, an...  15.4 us
    ppermute x5, waiting for transfers between devices, gather_pieces(): held = jnp.concatenate([held, lax.ppermute(held, axis, pairs)], axis=0)  11 us
    pallas_call x1, Pallas kernels, local(): pl.pallas_call(lambda *refs: down_kernel(height, total, spacings, *refs),...  10.3 us
    ppermute x4, starting transfers between devices, spread(): return (lax.ppermute(last, 'rad', up), lax.ppermute(leading, 'rad', down))  9.18 us
    ppermute x5, starting transfers between devices, gather_pieces(): held = jnp.concatenate([held, lax.ppermute(held, axis, pairs)], axis=0)  7.88 us
    ppermute x1, starting transfers between devices, local(): before = lax.ppermute(last, 'ang', ring_up)  3.02 us
    ppermute x4, waiting for transfers between devices, spread(): return (lax.ppermute(last, 'rad', up), lax.ppermute(leading, 'rad', down))  2.9 us
  transfers between devices with their start and end apart: 11, of which 6 were waited for; matrix products, arithmetic and copies ran while one was open for 3% of the time, Pallas kernels for 0%

profile of v3, /device:TPU:0, one launch (start us, length us, event | category | flops | bytes accessed | tf_op | source)
XLA Modules:
  0.0 64.6 jit_solution(10267219612955089040)
XLA Ops:
  0.6 0.0 copy-start
  0.6 1.1 %fusion.6 = (f32[128,64]{1,0:T(8,128)S(1)}, f32[128,64]{1,0:T(8,128)S(1)}, f32[128,64]{1,0:T(8,128)S(1)}, f32[128,64]{1,0:T(8,128)S(1)}) fusion(f32[128,1024]{1,0:T(8,128)} %refs_1_.1, f32[128,1024]{1,0:T(8,128)} %refs_3_.1), kind=kLoop, calls=%fused_computation.37 | loop fusion | bytes 262144 | tf_op jit(solution)/shard_map/slice | solution.py:371
  1.7 0.1 pad_maximum_fusion.3
  1.8 3.0 %collective-permute-start.1 = (f32[128,128]{1,0:T(8,128)S(1)}, f32[128,128]{1,0:T(8,128)S(1)}, u32[]{:S(2)}, u32[]{:S(2)}) collective-permute-start(f32[128,128]{1,0:T(8,128)S(1)} %pad_maximum_fusion.3), channel_id=1, source_target_pairs={{0,8},{8,16},{16,24},{24,0},{1,9},{9,17},{17,25},{25,1},{2,10},{10... | collective-permute-start | bytes 196616 | tf_op jit(solution)/shard_map/ppermute | solution.py:374
  4.8 0.1 pad_maximum_fusion.2
  4.9 1.0 %collective-permute-start = (f32[128,128]{1,0:T(8,128)S(1)}, f32[128,128]{1,0:T(8,128)S(1)}, u32[]{:S(2)}, u32[]{:S(2)}) collective-permute-start(f32[128,128]{1,0:T(8,128)S(1)} %pad_maximum_fusion.2), channel_id=1, source_target_pairs={{8,0},{16,8},{24,16},{0,24},{9,1},{17,9},{25,17},{1,25},{10,2},{18... | collective-permute-start | bytes 196616 | tf_op jit(solution)/shard_map/ppermute | solution.py:373
  6.0 0.0 copy-done
  6.0 1.1 %fusion.4 = (f32[64,1024]{1,0:T(8,128)S(1)}, f32[64,1024]{1,0:T(8,128)S(1)}, f32[64,1024]{1,0:T(8,128)S(1)}, f32[64,1024]{1,0:T(8,128)S(1)}) fusion(f32[128,1024]{1,0:T(8,128)S(1)} %copy-done, f32[128,1024]{1,0:T(8,128)} %refs_3_.1), kind=kLoop, calls=%fused_computation.35 | loop fusion | bytes 2097152 | tf_op jit(solution)/shard_map/slice | solution.py:367
  7.1 1.5 %collective-permute-start.2 = (f32[128,1024]{1,0:T(8,128)S(1)}, f32[128,1024]{1,0:T(8,128)S(1)}, u32[]{:S(2)}, u32[]{:S(2)}) collective-permute-start(f32[128,1024]{1,0:T(8,128)S(1)} %pad_maximum_fusion), channel_id=1, source_target_pairs={{0,1},{1,2},{2,3},{3,4},{4,5},{5,6},{6,7},{8,9},{9,10},{10,11},{11... | collective-permute-start | bytes 1572872 | tf_op jit(solution)/shard_map/ppermute | solution.py:368
  8.7 1.3 %collective-permute-start.3 = (f32[128,1024]{1,0:T(8,128)S(1)}, f32[128,1024]{1,0:T(8,128)S(1)}, u32[]{:S(2)}, u32[]{:S(2)}) collective-permute-start(f32[128,1024]{1,0:T(8,128)S(1)} %pad_maximum_fusion.1), channel_id=1, source_target_pairs={{1,0},{2,1},{3,2},{4,3},{5,4},{6,5},{7,6},{9,8},{10,9},{11,10},{12... | collective-permute-start | bytes 1572872 | tf_op jit(solution)/shard_map/ppermute | solution.py:368
  10.0 0.1 pad_add_fusion.refs_0_
  10.1 0.0 collective-permute-done.1
  10.1 0.1 fusion.9
  10.2 0.0 collective-permute-done
  10.2 0.1 fusion.8
  10.2 0.0 copy-start.1
  10.2 0.1 fusion.1
  10.3 0.1 fusion.3
  10.5 5.1 %collective-permute-start.4 = (f32[128,128]{1,0:T(8,128)S(1)}, f32[128,128]{1,0:T(8,128)S(1)}, u32[]{:S(2)}, u32[]{:S(2)}) collective-permute-start(f32[128,128]{1,0:T(8,128)S(1)} %pad_maximum_fusion.4), channel_id=1, source_target_pairs={{0,1},{1,2},{2,3},{3,4},{4,5},{5,6},{6,7},{8,9},{9,10},{10,11},{11... | collective-permute-start | bytes 196616 | tf_op jit(solution)/shard_map/ppermute | solution.py:368
  15.6 1.3 %collective-permute-start.5 = (f32[128,128]{1,0:T(8,128)S(1)}, f32[128,128]{1,0:T(8,128)S(1)}, u32[]{:S(2)}, u32[]{:S(2)}) collective-permute-start(f32[128,128]{1,0:T(8,128)S(1)} %pad_maximum_fusion.5), channel_id=1, source_target_pairs={{1,0},{2,1},{3,2},{4,3},{5,4},{6,5},{7,6},{9,8},{10,9},{11,10},{12... | collective-permute-start | bytes 196616 | tf_op jit(solution)/shard_map/ppermute | solution.py:368
  16.9 0.1 pad_maximum_fusion.8.refs_4_
  17.0 0.1 pad_maximum_fusion.7.refs_2_
  17.1 0.0 collective-permute-done.4.refs_7_
  17.1 2.9 %collective-permute-done.5.refs_8_ = f32[128,128]{1,0:T(8,128)S(1)} collective-permute-done((f32[128,128]{1,0:T(8,128)S(1)}, f32[128,128]{1,0:T(8,128)S(1)}, u32[]{:S(2)}, u32[]{:S(2)}) %collective-permute-start.5) | collective-permute-done | bytes 65568 | tf_op jit(solution)/shard_map/ppermute | solution.py:368
  20.0 0.0 collective-permute-done.2.refs_5_
  20.0 0.0 collective-permute-done.3.refs_6_
  20.0 0.0 copy-done.1
  20.0 10.3 %down.1 = (f32[144,1152]{1,0:T(8,128)S(1)}, f32[144,1152]{1,0:T(8,128)}, f32[80,640]{1,0:T(8,128)S(1)}, f32[80,640]{1,0:T(8,128)S(1)}, f32[48,384]{1,0:T(8,128)S...) custom-call(s32[2]{0:T(128)S(1)} %pad_add_fusion.refs_0_, f32[128,1024]{1,0:T(8,128)S(1)} %copy-done, ...), custom_call_target="tpu_custom_call" | custom-call | tf_op jit(solution)/shard_map/down/pallas_call | solution.py:389
  30.3 0.0 copy-start.2
  30.3 3.8 %collective-permute-start.6 = (f32[1,16,128]{2,1,0:T(8,128)S(1)}, f32[1,16,128]{2,1,0:T(8,128)S(1)}, u32[]{:S(2)}, u32[]{:S(2)}) collective-permute-start(f32[1,16,128]{2,1,0:T(8,128)S(1)} %bitcast.5), channel_id=1, source_target_pairs={{0,4},{1,5},{2,6},{3,7},{4,0},{5,1},{6,2},{7,3},{8,12},{9,13},{10,... | collective-permute-start | bytes 24584 | tf_op jit(solution)/shard_map/ppermute | solution.py:342
  34.1 1.6 %collective-permute-done.6 = f32[1,16,128]{2,1,0:T(8,128)S(1)} collective-permute-done((f32[1,16,128]{2,1,0:T(8,128)S(1)}, f32[1,16,128]{2,1,0:T(8,128)S(1)}, u32[]{:S(2)}, u32[]{:S(2)}) %collective-permute-start.6) | collective-permute-done | bytes 8224 | tf_op jit(solution)/shard_map/ppermute | solution.py:342
  35.7 1.9 %collective-permute-start.7 = (f32[2,16,128]{2,1,0:T(8,128)S(1)}, f32[2,16,128]{2,1,0:T(8,128)S(1)}, u32[]{:S(2)}, u32[]{:S(2)}) collective-permute-start(f32[2,16,128]{2,1,0:T(8,128)S(1)} %pad_maximum_fusion.10), channel_id=1, source_target_pairs={{0,2},{1,3},{2,0},{3,1},{4,6},{5,7},{6,4},{7,5},{8,10},{9,11},{10,... | collective-permute-start | bytes 49160 | tf_op jit(solution)/shard_map/ppermute | solution.py:342
  37.6 1.9 %collective-permute-done.7 = f32[2,16,128]{2,1,0:T(8,128)S(1)} collective-permute-done((f32[2,16,128]{2,1,0:T(8,128)S(1)}, f32[2,16,128]{2,1,0:T(8,128)S(1)}, u32[]{:S(2)}, u32[]{:S(2)}) %collective-permute-start.7) | collective-permute-done | bytes 16416 | tf_op jit(solution)/shard_map/ppermute | solution.py:342
  39.5 0.6 collective-permute-start.8
  40.1 3.3 %collective-permute-done.8 = f32[4,16,128]{2,1,0:T(8,128)S(1)} collective-permute-done((f32[4,16,128]{2,1,0:T(8,128)S(1)}, f32[4,16,128]{2,1,0:T(8,128)S(1)}, u32[]{:S(2)}, u32[]{:S(2)}) %collective-permute-start.8) | collective-permute-done | bytes 32800 | tf_op jit(solution)/shard_map/ppermute | solution.py:342
  43.5 1.5 %collective-permute-start.9 = (f32[8,16,128]{2,1,0:T(8,128)S(1)}, f32[8,16,128]{2,1,0:T(8,128)S(1)}, u32[]{:S(2)}, u32[]{:S(2)}) collective-permute-start(f32[8,16,128]{2,1,0:T(8,128)S(1)} %pad_maximum_fusion.6), channel_id=1, source_target_pairs={{0,16},{8,24},{16,0},{24,8},{1,17},{9,25},{17,1},{25,9},{2,18},{10... | collective-permute-start | bytes 196616 | tf_op jit(solution)/shard_map/ppermute | solution.py:342
  45.0 2.7 %collective-permute-done.9 = f32[8,16,128]{2,1,0:T(8,128)S(1)} collective-permute-done((f32[8,16,128]{2,1,0:T(8,128)S(1)}, f32[8,16,128]{2,1,0:T(8,128)S(1)}, u32[]{:S(2)}, u32[]{:S(2)}) %collective-permute-start.9) | collective-permute-done | bytes 65568 | tf_op jit(solution)/shard_map/ppermute | solution.py:342
  47.8 0.1 collective-permute-start.10
  47.8 1.3 %collective-permute-done.10 = f32[16,16,128]{2,1,0:T(8,128)S(1)} collective-permute-done((f32[16,16,128]{2,1,0:T(8,128)S(1)}, f32[16,16,128]{2,1,0:T(8,128)S(1)}, u32[]{:S(2)}, u32[]{:S(2)}) %collective-permute-start.10) | collective-permute-done | bytes 131104 | tf_op jit(solution)/shard_map/ppermute | solution.py:342
  49.2 0.0 copy-done.2
  49.2 15.4 %up.1 = (f32[128,1024]{1,0:T(8,128)}, f32[128,1024]{1,0:T(8,128)}) custom-call(s32[2]{0:T(128)S(1)} %pad_add_fusion.refs_0_, f32[32,16,128]{2,1,0:T(8,128)S(1)} %constant_dynamic-update-slice_fusion.5.refs_1_, f32[144,1152]{1,0:T(8,128)S(1)} %get-tuple-element.10.refs_2_, f32[144,1152]{1,0:T(8,128)S(1)} %copy-done.2, ...), custom_call_target="tpu_custom_call" | custom-call | tf_op jit(solution)/shard_map/up/pallas_call | solution.py:409
  (13 shorter events, 0.1 us)
Async XLA Ops:
  0.6 5.3 %copy-start = (f32[128,1024]{1,0:T(8,128)S(1)}, f32[128,1024]{1,0:T(8,128)}, u32[]{:S(2)}) copy-start(f32[128,1024]{1,0:T(8,128)} %refs_1_.1) | copy-start | bytes 1572868
  1.8 8.2 %collective-permute-start.1 = (f32[128,128]{1,0:T(8,128)S(1)}, f32[128,128]{1,0:T(8,128)S(1)}, u32[]{:S(2)}, u32[]{:S(2)}) collective-permute-start(f32[128,128]{1,0:T(8,128)S(1)} %pad_maximum_fusion.3), channel_id=1, source_target_pairs={{0,8},{8,16},{16,24},{24,0},{1,9},{9,17},{17,25},{25,1},{2,10},{10... | collective-permute-start | bytes 196616 | tf_op jit(solution)/shard_map/ppermute | solution.py:374
  4.9 5.2 %collective-permute-start = (f32[128,128]{1,0:T(8,128)S(1)}, f32[128,128]{1,0:T(8,128)S(1)}, u32[]{:S(2)}, u32[]{:S(2)}) collective-permute-start(f32[128,128]{1,0:T(8,128)S(1)} %pad_maximum_fusion.2), channel_id=1, source_target_pairs={{8,0},{16,8},{24,16},{0,24},{9,1},{17,9},{25,17},{1,25},{10,2},{18... | collective-permute-start | bytes 196616 | tf_op jit(solution)/shard_map/ppermute | solution.py:373
  7.1 12.8 %collective-permute-start.2 = (f32[128,1024]{1,0:T(8,128)S(1)}, f32[128,1024]{1,0:T(8,128)S(1)}, u32[]{:S(2)}, u32[]{:S(2)}) collective-permute-start(f32[128,1024]{1,0:T(8,128)S(1)} %pad_maximum_fusion), channel_id=1, source_target_pairs={{0,1},{1,2},{2,3},{3,4},{4,5},{5,6},{6,7},{8,9},{9,10},{10,11},{11... | collective-permute-start | bytes 1572872 | tf_op jit(solution)/shard_map/ppermute | solution.py:368
  8.7 11.3 %collective-permute-start.3 = (f32[128,1024]{1,0:T(8,128)S(1)}, f32[128,1024]{1,0:T(8,128)S(1)}, u32[]{:S(2)}, u32[]{:S(2)}) collective-permute-start(f32[128,1024]{1,0:T(8,128)S(1)} %pad_maximum_fusion.1), channel_id=1, source_target_pairs={{1,0},{2,1},{3,2},{4,3},{5,4},{6,5},{7,6},{9,8},{10,9},{11,10},{12... | collective-permute-start | bytes 1572872 | tf_op jit(solution)/shard_map/ppermute | solution.py:368
  10.2 9.7 %copy-start.1 = (f32[128,1024]{1,0:T(8,128)S(1)}, f32[128,1024]{1,0:T(8,128)}, u32[]{:S(2)}) copy-start(f32[128,1024]{1,0:T(8,128)} %refs_3_.1) | copy-start | bytes 1572868
  10.5 6.6 %collective-permute-start.4 = (f32[128,128]{1,0:T(8,128)S(1)}, f32[128,128]{1,0:T(8,128)S(1)}, u32[]{:S(2)}, u32[]{:S(2)}) collective-permute-start(f32[128,128]{1,0:T(8,128)S(1)} %pad_maximum_fusion.4), channel_id=1, source_target_pairs={{0,1},{1,2},{2,3},{3,4},{4,5},{5,6},{6,7},{8,9},{9,10},{10,11},{11... | collective-permute-start | bytes 196616 | tf_op jit(solution)/shard_map/ppermute | solution.py:368
  15.6 4.4 %collective-permute-start.5 = (f32[128,128]{1,0:T(8,128)S(1)}, f32[128,128]{1,0:T(8,128)S(1)}, u32[]{:S(2)}, u32[]{:S(2)}) collective-permute-start(f32[128,128]{1,0:T(8,128)S(1)} %pad_maximum_fusion.5), channel_id=1, source_target_pairs={{1,0},{2,1},{3,2},{4,3},{5,4},{6,5},{7,6},{9,8},{10,9},{11,10},{12... | collective-permute-start | bytes 196616 | tf_op jit(solution)/shard_map/ppermute | solution.py:368
  30.3 18.9 %copy-start.2 = (f32[144,1152]{1,0:T(8,128)S(1)}, f32[144,1152]{1,0:T(8,128)}, u32[]{:S(2)}) copy-start(f32[144,1152]{1,0:T(8,128)} %get-tuple-element.11.refs_3_) | copy-start | bytes 1990660
  30.3 5.4 %collective-permute-start.6 = (f32[1,16,128]{2,1,0:T(8,128)S(1)}, f32[1,16,128]{2,1,0:T(8,128)S(1)}, u32[]{:S(2)}, u32[]{:S(2)}) collective-permute-start(f32[1,16,128]{2,1,0:T(8,128)S(1)} %bitcast.5), channel_id=1, source_target_pairs={{0,4},{1,5},{2,6},{3,7},{4,0},{5,1},{6,2},{7,3},{8,12},{9,13},{10,... | collective-permute-start | bytes 24584 | tf_op jit(solution)/shard_map/ppermute | solution.py:342
  35.7 3.9 %collective-permute-start.7 = (f32[2,16,128]{2,1,0:T(8,128)S(1)}, f32[2,16,128]{2,1,0:T(8,128)S(1)}, u32[]{:S(2)}, u32[]{:S(2)}) collective-permute-start(f32[2,16,128]{2,1,0:T(8,128)S(1)} %pad_maximum_fusion.10), channel_id=1, source_target_pairs={{0,2},{1,3},{2,0},{3,1},{4,6},{5,7},{6,4},{7,5},{8,10},{9,11},{10,... | collective-permute-start | bytes 49160 | tf_op jit(solution)/shard_map/ppermute | solution.py:342
  39.5 3.9 %collective-permute-start.8 = (f32[4,16,128]{2,1,0:T(8,128)S(1)}, f32[4,16,128]{2,1,0:T(8,128)S(1)}, u32[]{:S(2)}, u32[]{:S(2)}) collective-permute-start(f32[4,16,128]{2,1,0:T(8,128)S(1)} %pad_maximum_fusion.9), channel_id=1, source_target_pairs={{0,8},{8,0},{16,24},{24,16},{1,9},{9,1},{17,25},{25,17},{2,10},{10... | collective-permute-start | bytes 98312 | tf_op jit(solution)/shard_map/ppermute | solution.py:342
  43.5 4.3 %collective-permute-start.9 = (f32[8,16,128]{2,1,0:T(8,128)S(1)}, f32[8,16,128]{2,1,0:T(8,128)S(1)}, u32[]{:S(2)}, u32[]{:S(2)}) collective-permute-start(f32[8,16,128]{2,1,0:T(8,128)S(1)} %pad_maximum_fusion.6), channel_id=1, source_target_pairs={{0,16},{8,24},{16,0},{24,8},{1,17},{9,25},{17,1},{25,9},{2,18},{10... | collective-permute-start | bytes 196616 | tf_op jit(solution)/shard_map/ppermute | solution.py:342
  47.8 1.4 %collective-permute-start.10 = (f32[16,16,128]{2,1,0:T(8,128)S(1)}, f32[16,16,128]{2,1,0:T(8,128)S(1)}, u32[]{:S(2)}, u32[]{:S(2)}) collective-permute-start(f32[16,16,128]{2,1,0:T(8,128)S(1)} %get-tuple-element.28), channel_id=1, source_target_pairs={{0,1},{1,0},{2,3},{3,2},{4,5},{5,4},{6,7},{7,6},{8,9},{9,8},{10,11... | collective-permute-start | bytes 393224 | tf_op jit(solution)/shard_map/ppermute | solution.py:342

commit v4 on v3

--- a/solution.py
+++ b/solution.py
@@ -374,7 +374,20 @@
     before = lax.ppermute(last, "ang", ring_up)
     halo_v = jnp.concatenate([after[:, :SIDE], before[:, :SIDE]], axis=1)
     halo_g = jnp.concatenate([after[:, SIDE:], before[:, SIDE:]], axis=1)
-    corner_above, corner_below = spread(halo_v, halo_g)
+
+    def corner(strip_first, strip_last, step):
+        rows = range(rads - 1) if step > 0 else range(1, rads)
+        moves = [(r, (a + 1) % angs, a) for r in rows for a in range(angs)]
+        from_after = [(b * rads + r, a * rads + r + step) for r, b, a in moves]
+        from_before = [(a * rads + r, b * rads + r + step) for r, b, a in moves]
+        right = lax.ppermute(strip_first, ("ang", "rad"), from_after)
+        left = lax.ppermute(strip_last, ("ang", "rad"), from_before)
+        top = jnp.concatenate([right[:, :SIDE], left[:, :SIDE]], axis=1)
+        low = jnp.concatenate([right[:, SIDE:], left[:, SIDE:]], axis=1)
+        return jnp.concatenate([top, low], axis=0)
+
+    corner_above = corner(first[-halo:], last[-halo:], 1)
+    corner_below = corner(first[:halo], last[:halo], -1)
     place = jnp.stack([lax.axis_index("rad"), lax.axis_index("ang")]).astype(jnp.int32)
     smem = pl.BlockSpec(memory_space=pltpu.SMEM)
     full = pl.BlockSpec(memory_space=pltpu.VMEM)

time: 64.8 us -> 75.3 us (1.16)
  starting transfers between devices: 21.1 us -> 32.8 us
  waiting for transfers between devices: 13.9 us -> 13.1 us
    ppermute x0 -> x4, starting transfers between devices: none -> 13.8 us  [the longest x2 8.12 us: corner(): right = lax.ppermute(strip_first, ('ang', 'rad'), from_after)]
    ppermute x4 -> x2, starting transfers between devices: 9.18 us -> 4.29 us  [spread(): return (lax.ppermute(last, 'rad', up), lax.ppermute(leading, 'rad', down))]
    ppermute x5, starting transfers between devices: 7.88 us -> 11.7 us  [gather_pieces(): held = jnp.concatenate([held, lax.ppermute(held, axis, pairs)], axis=0)]
    ppermute x1, starting transfers between devices: 3.02 us -> 1.39 us  [local(): before = lax.ppermute(last, 'ang', ring_up)]
    ppermute x4 -> x2, waiting for transfers between devices: 2.9 us -> 1.87 us  [spread(): return (lax.ppermute(last, 'rad', up), lax.ppermute(leading, 'rad', down))]
    slice x1, local copies, waits for them, and re-layouts: 1.13 us -> 0.1 us  [spread(): leading = jnp.concatenate([x[:halo], y[:halo]], axis=0)]
  transfers between devices with their start and end apart: 11 -> 13, of which waited for: 6 -> 6; matrix products, arithmetic and copies ran while one was open for 3% -> 2% of each run, Pallas kernels for 0% -> 0%
where the time goes in v4:
time: 75.3 us; the launch traced here: 75 us
  starting transfers between devices  32.8 us (44%)
  Pallas kernels  25.7 us (34%)
  waiting for transfers between devices  13.1 us (17%)
  local copies, waits for them, and re-layouts  1.69 us (2%)
  between operations  0.88 us (1%)
  other arithmetic  0.84 us (1%)
    pallas_call x1, Pallas kernels, local(): pl.pallas_call(lambda *refs: up_kernel(height, total, spacings, (rads, an...  15.4 us
    ppermute x5, starting transfers between devices, gather_pieces(): held = jnp.concatenate([held, lax.ppermute(held, axis, pairs)], axis=0)  11.7 us
    ppermute x5, waiting for transfers between devices, gather_pieces(): held = jnp.concatenate([held, lax.ppermute(held, axis, pairs)], axis=0)  11.3 us
    pallas_call x1, Pallas kernels, local(): pl.pallas_call(lambda *refs: down_kernel(height, total, spacings, *refs),...  10.3 us
    ppermute x2, starting transfers between devices, corner(): right = lax.ppermute(strip_first, ('ang', 'rad'), from_after)  8.12 us
    ppermute x2, starting transfers between devices, corner(): left = lax.ppermute(strip_last, ('ang', 'rad'), from_before)  5.66 us
    ppermute x2, starting transfers between devices, spread(): return (lax.ppermute(last, 'rad', up), lax.ppermute(leading, 'rad', down))  4.29 us
    ppermute x2, waiting for transfers between devices, spread(): return (lax.ppermute(last, 'rad', up), lax.ppermute(leading, 'rad', down))  1.87 us
  transfers between devices with their start and end apart: 13, of which 6 were waited for; matrix products, arithmetic and copies ran while one was open for 2% of the time, Pallas kernels for 0%

profile of v4, /device:TPU:0, one launch (start us, length us, event | category | flops | bytes accessed | tf_op | source)
XLA Modules:
  0.0 75.0 jit_solution(9340340691830891316)
XLA Ops:
  0.6 0.0 copy-start.1
  0.6 1.1 %fusion.6 = (f32[128,64]{1,0:T(8,128)S(1)}, f32[128,64]{1,0:T(8,128)S(1)}, f32[128,64]{1,0:T(8,128)S(1)}, f32[128,64]{1,0:T(8,128)S(1)}) fusion(f32[128,1024]{1,0:T(8,128)} %refs_1_.1, f32[128,1024]{1,0:T(8,128)} %refs_3_.1), kind=kLoop, calls=%fused_computation.37 | loop fusion | bytes 262144 | tf_op jit(solution)/shard_map/slice | solution.py:371
  1.7 0.0 copy-start
  1.7 0.1 fusion.3
  1.8 1.4 %collective-permute-start.6 = (f32[64,128]{1,0:T(8,128)S(1)}, f32[64,128]{1,0:T(8,128)S(1)}, u32[]{:S(2)}, u32[]{:S(2)}) collective-permute-start(f32[64,128]{1,0:T(8,128)S(1)} %get-tuple-element.24), channel_id=1, source_target_pairs={{9,0},{17,8},{25,16},{1,24},{10,1},{18,9},{26,17},{2,25},{11,2},{1... | collective-permute-start | bytes 98312 | tf_op jit(solution)/shard_map/ppermute | solution.py:383
  3.3 6.7 %collective-permute-start.4 = (f32[64,128]{1,0:T(8,128)S(1)}, f32[64,128]{1,0:T(8,128)S(1)}, u32[]{:S(2)}, u32[]{:S(2)}) collective-permute-start(f32[64,128]{1,0:T(8,128)S(1)} %get-tuple-element.25), channel_id=1, source_target_pairs={{8,1},{16,9},{24,17},{0,25},{9,2},{17,10},{25,18},{1,26},{10,3},{1... | collective-permute-start | bytes 98312 | tf_op jit(solution)/shard_map/ppermute | solution.py:383
  10.0 0.1 fusion.1
  10.1 1.3 %collective-permute-start.7 = (f32[64,128]{1,0:T(8,128)S(1)}, f32[64,128]{1,0:T(8,128)S(1)}, u32[]{:S(2)}, u32[]{:S(2)}) collective-permute-start(f32[64,128]{1,0:T(8,128)S(1)} %get-tuple-element.26), channel_id=1, source_target_pairs={{1,8},{9,16},{17,24},{25,0},{2,9},{10,17},{18,25},{26,1},{3,10},{1... | collective-permute-start | bytes 98312 | tf_op jit(solution)/shard_map/ppermute | solution.py:384
  11.4 4.4 %collective-permute-start.5 = (f32[64,128]{1,0:T(8,128)S(1)}, f32[64,128]{1,0:T(8,128)S(1)}, u32[]{:S(2)}, u32[]{:S(2)}) collective-permute-start(f32[64,128]{1,0:T(8,128)S(1)} %get-tuple-element.27), channel_id=1, source_target_pairs={{0,9},{8,17},{16,25},{24,1},{1,10},{9,18},{17,26},{25,2},{2,11},{1... | collective-permute-start | bytes 98312 | tf_op jit(solution)/shard_map/ppermute | solution.py:384
  15.7 0.1 pad_maximum_fusion.6
  15.8 1.4 %collective-permute-start.1 = (f32[128,128]{1,0:T(8,128)S(1)}, f32[128,128]{1,0:T(8,128)S(1)}, u32[]{:S(2)}, u32[]{:S(2)}) collective-permute-start(f32[128,128]{1,0:T(8,128)S(1)} %pad_maximum_fusion.6), channel_id=1, source_target_pairs={{0,8},{8,16},{16,24},{24,0},{1,9},{9,17},{17,25},{25,1},{2,10},{10... | collective-permute-start | bytes 196616 | tf_op jit(solution)/shard_map/ppermute | solution.py:374
  17.2 0.1 pad_maximum_fusion.5
  17.3 0.0 copy-done.1
  17.3 0.0 copy-done
  17.3 0.1 fusion.4
  17.5 0.1 pad_add_fusion.refs_0_
  17.6 0.0 collective-permute-done.6
  17.6 1.6 %collective-permute-start = (f32[128,128]{1,0:T(8,128)S(1)}, f32[128,128]{1,0:T(8,128)S(1)}, u32[]{:S(2)}, u32[]{:S(2)}) collective-permute-start(f32[128,128]{1,0:T(8,128)S(1)} %pad_maximum_fusion.5), channel_id=1, source_target_pairs={{8,0},{16,8},{24,16},{0,24},{9,1},{17,9},{25,17},{1,25},{10,2},{18... | collective-permute-start | bytes 196616 | tf_op jit(solution)/shard_map/ppermute | solution.py:373
  19.2 0.1 fusion.10
  19.3 0.0 collective-permute-done.4
  19.3 3.0 %collective-permute-start.2 = (f32[128,1024]{1,0:T(8,128)S(1)}, f32[128,1024]{1,0:T(8,128)S(1)}, u32[]{:S(2)}, u32[]{:S(2)}) collective-permute-start(f32[128,1024]{1,0:T(8,128)S(1)} %pad_maximum_fusion), channel_id=1, source_target_pairs={{0,1},{1,2},{2,3},{3,4},{4,5},{5,6},{6,7},{8,9},{9,10},{10,11},{11... | collective-permute-start | bytes 1572872 | tf_op jit(solution)/shard_map/ppermute | solution.py:368
  22.3 0.1 fusion.12
  22.4 0.0 collective-permute-done.7
  22.4 1.3 %collective-permute-start.3 = (f32[128,1024]{1,0:T(8,128)S(1)}, f32[128,1024]{1,0:T(8,128)S(1)}, u32[]{:S(2)}, u32[]{:S(2)}) collective-permute-start(f32[128,1024]{1,0:T(8,128)S(1)} %pad_maximum_fusion.1), channel_id=1, source_target_pairs={{1,0},{2,1},{3,2},{4,3},{5,4},{6,5},{7,6},{9,8},{10,9},{11,10},{12... | collective-permute-start | bytes 1572872 | tf_op jit(solution)/shard_map/ppermute | solution.py:368
  23.7 0.1 fusion.11
  23.7 0.1 maximum_maximum_fusion.1.refs_8_
  23.8 0.0 collective-permute-done.5
  23.8 0.1 fusion.13
  23.9 0.1 maximum_maximum_fusion.refs_7_
  24.0 0.0 collective-permute-done.1
  24.0 0.1 fusion.9
  24.1 0.0 collective-permute-done
  24.1 0.1 fusion.8
  24.2 0.1 pad_maximum_fusion.3.refs_4_
  24.3 0.1 pad_maximum_fusion.2.refs_2_
  24.4 0.0 collective-permute-done.2.refs_5_
  24.4 1.9 %collective-permute-done.3.refs_6_ = f32[128,1024]{1,0:T(8,128)S(1)} collective-permute-done((f32[128,1024]{1,0:T(8,128)S(1)}, f32[128,1024]{1,0:T(8,128)S(1)}, u32[]{:S(2)}, u32[]{:S(2)}) %collective-permute-start.3) | collective-permute-done | bytes 524320 | tf_op jit(solution)/shard_map/ppermute | solution.py:368
  26.3 10.3 %down.1 = (f32[144,1152]{1,0:T(8,128)S(1)}, f32[144,1152]{1,0:T(8,128)}, f32[80,640]{1,0:T(8,128)S(1)}, f32[80,640]{1,0:T(8,128)S(1)}, f32[48,384]{1,0:T(8,128)S...) custom-call(s32[2]{0:T(128)S(1)} %pad_add_fusion.refs_0_, f32[128,1024]{1,0:T(8,128)S(1)} %copy-done, ...), custom_call_target="tpu_custom_call" | custom-call | tf_op jit(solution)/shard_map/down/pallas_call | solution.py:402
  36.6 0.0 copy-start.2
  36.6 7.9 %collective-permute-start.8 = (f32[1,16,128]{2,1,0:T(8,128)S(1)}, f32[1,16,128]{2,1,0:T(8,128)S(1)}, u32[]{:S(2)}, u32[]{:S(2)}) collective-permute-start(f32[1,16,128]{2,1,0:T(8,128)S(1)} %bitcast.5), channel_id=1, source_target_pairs={{0,4},{1,5},{2,6},{3,7},{4,0},{5,1},{6,2},{7,3},{8,12},{9,13},{10,... | collective-permute-start | bytes 24584 | tf_op jit(solution)/shard_map/ppermute | solution.py:342
  44.5 1.6 %collective-permute-done.8 = f32[1,16,128]{2,1,0:T(8,128)S(1)} collective-permute-done((f32[1,16,128]{2,1,0:T(8,128)S(1)}, f32[1,16,128]{2,1,0:T(8,128)S(1)}, u32[]{:S(2)}, u32[]{:S(2)}) %collective-permute-start.8) | collective-permute-done | bytes 8224 | tf_op jit(solution)/shard_map/ppermute | solution.py:342
  46.1 1.9 %collective-permute-start.9 = (f32[2,16,128]{2,1,0:T(8,128)S(1)}, f32[2,16,128]{2,1,0:T(8,128)S(1)}, u32[]{:S(2)}, u32[]{:S(2)}) collective-permute-start(f32[2,16,128]{2,1,0:T(8,128)S(1)} %pad_maximum_fusion.8), channel_id=1, source_target_pairs={{0,2},{1,3},{2,0},{3,1},{4,6},{5,7},{6,4},{7,5},{8,10},{9,11},{10,... | collective-permute-start | bytes 49160 | tf_op jit(solution)/shard_map/ppermute | solution.py:342
  48.0 1.9 %collective-permute-done.9 = f32[2,16,128]{2,1,0:T(8,128)S(1)} collective-permute-done((f32[2,16,128]{2,1,0:T(8,128)S(1)}, f32[2,16,128]{2,1,0:T(8,128)S(1)}, u32[]{:S(2)}, u32[]{:S(2)}) %collective-permute-start.9) | collective-permute-done | bytes 16416 | tf_op jit(solution)/shard_map/ppermute | solution.py:342
  50.0 0.4 collective-permute-start.10
  50.4 3.5 %collective-permute-done.10 = f32[4,16,128]{2,1,0:T(8,128)S(1)} collective-permute-done((f32[4,16,128]{2,1,0:T(8,128)S(1)}, f32[4,16,128]{2,1,0:T(8,128)S(1)}, u32[]{:S(2)}, u32[]{:S(2)}) %collective-permute-start.10) | collective-permute-done | bytes 32800 | tf_op jit(solution)/shard_map/ppermute | solution.py:342
  53.9 1.4 %collective-permute-start.11 = (f32[8,16,128]{2,1,0:T(8,128)S(1)}, f32[8,16,128]{2,1,0:T(8,128)S(1)}, u32[]{:S(2)}, u32[]{:S(2)}) collective-permute-start(f32[8,16,128]{2,1,0:T(8,128)S(1)} %pad_maximum_fusion.4), channel_id=1, source_target_pairs={{0,16},{8,24},{16,0},{24,8},{1,17},{9,25},{17,1},{25,9},{2,18},{10... | collective-permute-start | bytes 196616 | tf_op jit(solution)/shard_map/ppermute | solution.py:342
  55.3 2.9 %collective-permute-done.11 = f32[8,16,128]{2,1,0:T(8,128)S(1)} collective-permute-done((f32[8,16,128]{2,1,0:T(8,128)S(1)}, f32[8,16,128]{2,1,0:T(8,128)S(1)}, u32[]{:S(2)}, u32[]{:S(2)}) %collective-permute-start.11) | collective-permute-done | bytes 65568 | tf_op jit(solution)/shard_map/ppermute | solution.py:342
  58.2 0.1 collective-permute-start.12
  58.3 1.3 %collective-permute-done.12 = f32[16,16,128]{2,1,0:T(8,128)S(1)} collective-permute-done((f32[16,16,128]{2,1,0:T(8,128)S(1)}, f32[16,16,128]{2,1,0:T(8,128)S(1)}, u32[]{:S(2)}, u32[]{:S(2)}) %collective-permute-start.12) | collective-permute-done | bytes 131104 | tf_op jit(solution)/shard_map/ppermute | solution.py:342
  59.6 0.0 copy-done.2
  59.6 15.4 %up.1 = (f32[128,1024]{1,0:T(8,128)}, f32[128,1024]{1,0:T(8,128)}) custom-call(s32[2]{0:T(128)S(1)} %pad_add_fusion.refs_0_, f32[32,16,128]{2,1,0:T(8,128)S(1)} %constant_dynamic-update-slice_fusion.5.refs_1_, f32[144,1152]{1,0:T(8,128)S(1)} %get-tuple-element.10.refs_2_, f32[144,1152]{1,0:T(8,128)S(1)} %copy-done.2, ...), custom_call_target="tpu_custom_call" | custom-call | tf_op jit(solution)/shard_map/up/pallas_call | solution.py:422
  (11 shorter events, 0.1 us)
Async XLA Ops:
  0.6 16.7 %copy-start.1 = (f32[128,1024]{1,0:T(8,128)S(1)}, f32[128,1024]{1,0:T(8,128)}, u32[]{:S(2)}) copy-start(f32[128,1024]{1,0:T(8,128)} %refs_3_.1) | copy-start | bytes 1572868
  1.7 15.6 %copy-start = (f32[128,1024]{1,0:T(8,128)S(1)}, f32[128,1024]{1,0:T(8,128)}, u32[]{:S(2)}) copy-start(f32[128,1024]{1,0:T(8,128)} %refs_1_.1) | copy-start | bytes 1572868
  1.8 15.8 %collective-permute-start.6 = (f32[64,128]{1,0:T(8,128)S(1)}, f32[64,128]{1,0:T(8,128)S(1)}, u32[]{:S(2)}, u32[]{:S(2)}) collective-permute-start(f32[64,128]{1,0:T(8,128)S(1)} %get-tuple-element.24), channel_id=1, source_target_pairs={{9,0},{17,8},{25,16},{1,24},{10,1},{18,9},{26,17},{2,25},{11,2},{1... | collective-permute-start | bytes 98312 | tf_op jit(solution)/shard_map/ppermute | solution.py:383
  3.3 16.0 %collective-permute-start.4 = (f32[64,128]{1,0:T(8,128)S(1)}, f32[64,128]{1,0:T(8,128)S(1)}, u32[]{:S(2)}, u32[]{:S(2)}) collective-permute-start(f32[64,128]{1,0:T(8,128)S(1)} %get-tuple-element.25), channel_id=1, source_target_pairs={{8,1},{16,9},{24,17},{0,25},{9,2},{17,10},{25,18},{1,26},{10,3},{1... | collective-permute-start | bytes 98312 | tf_op jit(solution)/shard_map/ppermute | solution.py:383
  10.1 12.3 %collective-permute-start.7 = (f32[64,128]{1,0:T(8,128)S(1)}, f32[64,128]{1,0:T(8,128)S(1)}, u32[]{:S(2)}, u32[]{:S(2)}) collective-permute-start(f32[64,128]{1,0:T(8,128)S(1)} %get-tuple-element.26), channel_id=1, source_target_pairs={{1,8},{9,16},{17,24},{25,0},{2,9},{10,17},{18,25},{26,1},{3,10},{1... | collective-permute-start | bytes 98312 | tf_op jit(solution)/shard_map/ppermute | solution.py:384
  11.4 12.5 %collective-permute-start.5 = (f32[64,128]{1,0:T(8,128)S(1)}, f32[64,128]{1,0:T(8,128)S(1)}, u32[]{:S(2)}, u32[]{:S(2)}) collective-permute-start(f32[64,128]{1,0:T(8,128)S(1)} %get-tuple-element.27), channel_id=1, source_target_pairs={{0,9},{8,17},{16,25},{24,1},{1,10},{9,18},{17,26},{25,2},{2,11},{1... | collective-permute-start | bytes 98312 | tf_op jit(solution)/shard_map/ppermute | solution.py:384
  15.8 8.2 %collective-permute-start.1 = (f32[128,128]{1,0:T(8,128)S(1)}, f32[128,128]{1,0:T(8,128)S(1)}, u32[]{:S(2)}, u32[]{:S(2)}) collective-permute-start(f32[128,128]{1,0:T(8,128)S(1)} %pad_maximum_fusion.6), channel_id=1, source_target_pairs={{0,8},{8,16},{16,24},{24,0},{1,9},{9,17},{17,25},{25,1},{2,10},{10... | collective-permute-start | bytes 196616 | tf_op jit(solution)/shard_map/ppermute | solution.py:374
  17.6 6.5 %collective-permute-start = (f32[128,128]{1,0:T(8,128)S(1)}, f32[128,128]{1,0:T(8,128)S(1)}, u32[]{:S(2)}, u32[]{:S(2)}) collective-permute-start(f32[128,128]{1,0:T(8,128)S(1)} %pad_maximum_fusion.5), channel_id=1, source_target_pairs={{8,0},{16,8},{24,16},{0,24},{9,1},{17,9},{25,17},{1,25},{10,2},{18... | collective-permute-start | bytes 196616 | tf_op jit(solution)/shard_map/ppermute | solution.py:373
  19.3 5.1 %collective-permute-start.2 = (f32[128,1024]{1,0:T(8,128)S(1)}, f32[128,1024]{1,0:T(8,128)S(1)}, u32[]{:S(2)}, u32[]{:S(2)}) collective-permute-start(f32[128,1024]{1,0:T(8,128)S(1)} %pad_maximum_fusion), channel_id=1, source_target_pairs={{0,1},{1,2},{2,3},{3,4},{4,5},{5,6},{6,7},{8,9},{9,10},{10,11},{11... | collective-permute-start | bytes 1572872 | tf_op jit(solution)/shard_map/ppermute | solution.py:368
  22.4 3.9 %collective-permute-start.3 = (f32[128,1024]{1,0:T(8,128)S(1)}, f32[128,1024]{1,0:T(8,128)S(1)}, u32[]{:S(2)}, u32[]{:S(2)}) collective-permute-start(f32[128,1024]{1,0:T(8,128)S(1)} %pad_maximum_fusion.1), channel_id=1, source_target_pairs={{1,0},{2,1},{3,2},{4,3},{5,4},{6,5},{7,6},{9,8},{10,9},{11,10},{12... | collective-permute-start | bytes 1572872 | tf_op jit(solution)/shard_map/ppermute | solution.py:368
  36.6 23.0 %copy-start.2 = (f32[144,1152]{1,0:T(8,128)S(1)}, f32[144,1152]{1,0:T(8,128)}, u32[]{:S(2)}) copy-start(f32[144,1152]{1,0:T(8,128)} %get-tuple-element.11.refs_3_) | copy-start | bytes 1990660
  36.6 9.6 %collective-permute-start.8 = (f32[1,16,128]{2,1,0:T(8,128)S(1)}, f32[1,16,128]{2,1,0:T(8,128)S(1)}, u32[]{:S(2)}, u32[]{:S(2)}) collective-permute-start(f32[1,16,128]{2,1,0:T(8,128)S(1)} %bitcast.5), channel_id=1, source_target_pairs={{0,4},{1,5},{2,6},{3,7},{4,0},{5,1},{6,2},{7,3},{8,12},{9,13},{10,... | collective-permute-start | bytes 24584 | tf_op jit(solution)/shard_map/ppermute | solution.py:342
  46.1 3.8 %collective-permute-start.9 = (f32[2,16,128]{2,1,0:T(8,128)S(1)}, f32[2,16,128]{2,1,0:T(8,128)S(1)}, u32[]{:S(2)}, u32[]{:S(2)}) collective-permute-start(f32[2,16,128]{2,1,0:T(8,128)S(1)} %pad_maximum_fusion.8), channel_id=1, source_target_pairs={{0,2},{1,3},{2,0},{3,1},{4,6},{5,7},{6,4},{7,5},{8,10},{9,11},{10,... | collective-permute-start | bytes 49160 | tf_op jit(solution)/shard_map/ppermute | solution.py:342
  50.0 3.9 %collective-permute-start.10 = (f32[4,16,128]{2,1,0:T(8,128)S(1)}, f32[4,16,128]{2,1,0:T(8,128)S(1)}, u32[]{:S(2)}, u32[]{:S(2)}) collective-permute-start(f32[4,16,128]{2,1,0:T(8,128)S(1)} %pad_maximum_fusion.7), channel_id=1, source_target_pairs={{0,8},{8,0},{16,24},{24,16},{1,9},{9,1},{17,25},{25,17},{2,10},{10... | collective-permute-start | bytes 98312 | tf_op jit(solution)/shard_map/ppermute | solution.py:342
  53.9 4.3 %collective-permute-start.11 = (f32[8,16,128]{2,1,0:T(8,128)S(1)}, f32[8,16,128]{2,1,0:T(8,128)S(1)}, u32[]{:S(2)}, u32[]{:S(2)}) collective-permute-start(f32[8,16,128]{2,1,0:T(8,128)S(1)} %pad_maximum_fusion.4), channel_id=1, source_target_pairs={{0,16},{8,24},{16,0},{24,8},{1,17},{9,25},{17,1},{25,9},{2,18},{10... | collective-permute-start | bytes 196616 | tf_op jit(solution)/shard_map/ppermute | solution.py:342
  58.2 1.4 %collective-permute-start.12 = (f32[16,16,128]{2,1,0:T(8,128)S(1)}, f32[16,16,128]{2,1,0:T(8,128)S(1)}, u32[]{:S(2)}, u32[]{:S(2)}) collective-permute-start(f32[16,16,128]{2,1,0:T(8,128)S(1)} %get-tuple-element.28), channel_id=1, source_target_pairs={{0,1},{1,0},{2,3},{3,2},{4,5},{5,4},{6,7},{7,6},{8,9},{9,8},{10,11... | collective-permute-start | bytes 393224 | tf_op jit(solution)/shard_map/ppermute | solution.py:342
